TPU v7x, 256 devices: a whole 4x4x8 slice. The times are simulated.
256 devices in a mesh: dp: 32 (over y, x, core), mp: 8 (over z).
Axes of the slice: x: 4, y: 4, z: 8, core: 2. Of those that a mesh axis runs over, the one named last changes fastest.
Arguments:
- acts: bfloat16 [8192, 8192], P('dp', 'mp'), may hold values from -6 to 6
- grads: bfloat16 [8192, 28672], P('dp', 'mp'), may hold values from -6 to 6
- proj_in: bfloat16 [8192, 64], replicated, may hold values from -0.0625 to 0.0625
- block_vals: bfloat16 [128, 128, 64], replicated, may hold values from -0.046875 to 0.046875
- block_index: int32 [128], replicated, may hold values from 0 to 223, as said below
- assign: int32 [32, 256], P('dp'), may hold values from 0 to 255, each once within a row
Outputs:
- features: bfloat16 [8192, 4096], P(('dp', 'mp'))
- factor: float32 [8, 512, 512], P('mp')
Inputs may be any that keep to these rules, and one draw needn't show every extreme that they name: `block_index`: 128 distinct row blocks. Each row of assign names every example of its group once.
All inputs are finite; a program needn't handle non-finite values.
Results may differ from a plain program's by a relative error of at most 0.013.
Values may be sent and summed in bfloat16 or wider, within the bound.
No kernel may reach another device: no remote copies, remote signals or barrier semaphores. Data moves between devices by JAX's collectives and lax.ppermute only.
A program may use at most 64 MiB of HBM per device.

v0:
```python
import jax
import jax.numpy as jnp
from jax import lax
from jax.sharding import PartitionSpec as P

FB = 512


DAMPING = 0.05


def upper_factor(matrix):
    return jnp.swapaxes(jnp.linalg.cholesky(matrix), 1, 2)


def shards(acts, grads, proj_in, block_vals, block_index, assign):
    mp_count = lax.axis_size("mp")
    dp_count = lax.axis_size("dp")
    row_order = assign[0]
    ex_rows = acts.shape[0] // mp_count
    block_rows = block_vals.shape[1]
    moved_acts, moved_grads = (
        lax.all_to_all(acts[row_order], "mp", split_axis=0, concat_axis=1, tiled=True),
        lax.all_to_all(grads[row_order], "mp", split_axis=0, concat_axis=1, tiled=True),
    )
    in_full = jnp.dot(moved_acts, proj_in, preferred_element_type=jnp.float32)
    grid = moved_grads.reshape(ex_rows, -1, block_rows)
    picked = jnp.take(grid, block_index, axis=1)
    out_full = jnp.einsum("rtk,tko->ro", picked, block_vals, preferred_element_type=jnp.float32)
    in_coords = in_full.astype(jnp.bfloat16)
    out_coords = out_full.astype(jnp.bfloat16)
    outer = in_coords.astype(jnp.float32)[:, :, None] * out_coords.astype(jnp.float32)[:, None, :]
    features = outer.reshape(ex_rows, -1).astype(jnp.bfloat16)
    my_columns = lax.all_to_all(features, "mp", split_axis=1, concat_axis=0, tiled=True)
    group_rows = my_columns.shape[0]
    block_count = my_columns.shape[1] // FB
    column_blocks = my_columns.reshape(group_rows, block_count, FB)
    gram_blocks = jnp.einsum(
        "rbi,rbj->bij", column_blocks, column_blocks, preferred_element_type=jnp.float32
    )
    row_total = group_rows * dp_count
    identity = jnp.eye(FB, dtype=jnp.float32)
    summed = lax.psum(gram_blocks.astype(jnp.bfloat16), "dp").astype(jnp.float32)
    factor = upper_factor(summed / row_total + DAMPING * identity)
    return (features, factor)


def solution(mesh):
    return jax.shard_map(
        shards,
        mesh=mesh,
        in_specs=(P("dp", "mp"), P("dp", "mp"), P(), P(), P(), P("dp", None)),
        out_specs=(P(("dp", "mp"), None), P("mp", None, None)),
        check_vma=False,
    )
```

profile of v0, /device:TPU:1, one launch (start us, length us, event | category | flops | bytes accessed | tf_op | source)
XLA Modules:
  0.0 335.9 jit_solution(5575935236578113680)
XLA Ops:
  8.0 3.5 %gather_fusion = bf16[256,1024]{1,0:T(8,128)(2,1)} fusion(bf16[256,1024]{1,0:T(8,128)(2,1)} %param.6, s32[1024]{0:T(1024)S(1)} %pad_clamp_fusion.1), kind=kCustom, calls=%fused_computation | custom fusion | bytes 1049600 | tf_op jit(solution)/shard_map/gather | solution.py:23
  11.5 9.0 %all-to-all-start = ((bf16[8,32,1024]{2,1,0:T(8,128)(2,1)}), bf16[8,32,1024]{2,1,0:T(8,128)(2,1)S(1)}, u32[]{:S(2)}, u32[]{:S(2)}) async-start(bf16[8,32,1024]{2,1,0:T(8,128)(2,1)} %bitcast.2), calls=%async_computation | async-start | bytes 1048576 | tf_op jit(solution)/shard_map/all_to_all | solution.py:23
  20.5 6.5 %gather_fusion.1 = bf16[256,3584]{1,0:T(8,128)(2,1)} fusion(bf16[256,3584]{1,0:T(8,128)(2,1)} %param.7, s32[1024]{0:T(1024)S(1)} %pad_clamp_fusion.1), kind=kCustom, calls=%fused_computation.1 | custom fusion | bytes 3671040 | tf_op jit(solution)/shard_map/gather | solution.py:24
  27.0 11.5 %all-to-all-done = bf16[8,32,1024]{2,1,0:T(8,128)(2,1)S(1)} async-done(((bf16[8,32,1024]{2,1,0:T(8,128)(2,1)}), bf16[8,32,1024]{2,1,0:T(8,128)(2,1)S(1)}, u32[]{:S(2)}, u32[]{:S(2)}) %all-to-all-start) | async-done | bytes 524320 | tf_op jit(solution)/shard_map/all_to_all | solution.py:23
  38.4 4.4 %all-to-all-start.1 = ((bf16[8,32,3584]{2,1,0:T(8,128)(2,1)}), bf16[8,32,3584]{2,1,0:T(8,128)(2,1)}, u32[]{:S(2)}, u32[]{:S(2)}) async-start(bf16[8,32,3584]{2,1,0:T(8,128)(2,1)} %bitcast.97), calls=%async_computation.1 | async-start | bytes 3670016 | tf_op jit(solution)/shard_map/all_to_all | solution.py:24
  43.0 1.6 fusion.7
  44.6 41.4 %all-to-all-done.1 = bf16[8,32,3584]{2,1,0:T(8,128)(2,1)} async-done(((bf16[8,32,3584]{2,1,0:T(8,128)(2,1)}), bf16[8,32,3584]{2,1,0:T(8,128)(2,1)}, u32[]{:S(2)}, u32[]{:S(2)}) %all-to-all-start.1) | async-done | bytes 1835040 | tf_op jit(solution)/shard_map/all_to_all | solution.py:24
  86.0 3.7 %copy.34 = bf16[32,8,3584]{2,1,0:T(8,128)(2,1)} copy(bf16[32,8,3584]{2,0,1:T(8,128)(2,1)} %bitcast.5) | data formatting | bytes 3670016 | tf_op jit(solution)/shard_map/all_to_all | solution.py:24
  89.8 4.7 %reshape.220 = bf16[32,224,128]{2,1,0:T(8,128)(2,1)} reshape(bf16[32,8,3584]{2,1,0:T(8,128)(2,1)} %copy.34) | data formatting | bytes 3670016 | tf_op jit(solution)/shard_map/reshape | solution.py:27
  94.5 3.4 %copy.35 = bf16[32,224,128]{2,0,1:T(8,128)(2,1)} copy(bf16[32,224,128]{2,1,0:T(8,128)(2,1)} %reshape.220) | data formatting | bytes 3670016 | tf_op jit(solution)/shard_map/reshape | solution.py:27
  97.9 2.3 gather_fusion.2
  101.7 13.9 %all_to_all.48 = bf16[32,8,512]{2,0,1:T(8,128)(2,1)S(1)} all-to-all(bf16[32,8,512]{2,0,1:T(8,128)(2,1)S(1)} %copy.36), channel_id=1, replica_groups=mesh['dp'=32,'mp'=8] {'mp'}, dimensions={1} | all-to-all | bytes 524288 | tf_op jit(solution)/shard_map/all_to_all | solution.py:34
  117.9 112.0 %all-reduce.3.cloned.1.call-done = bf16[1,512,512]{1,2,0:T(8,128)(2,1)} async-done(((bf16[1,512,512]{1,2,0:T(8,128)(2,1)}), bf16[1,512,512]{1,2,0:T(8,128)(2,1)}) %all-reduce.3.cloned.1.call-update) | async-done | bytes 524304 | tf_op jit(solution)/shard_map/psum | solution.py:43
  229.8 2.2 select_add_fusion
  232.0 1.6 copy.38
  235.8 11.7 %custom-call.31 = f32[1,128,128]{2,1,0:T(8,128)S(1)} custom-call(f32[1,128,128]{2,1,0:T(8,128)S(1)} %cholesky.264), custom_call_target="Cholesky" | custom-call | tf_op jit(solution)/shard_map/jit(cholesky)/cholesky | solution.py:13
  248.3 9.8 %custom-call.32 = f32[1,1,128,128]{2,3,1,0:T(8,128)S(1)} custom-call(f32[1,1,128,128]{3,2,1,0:T(8,128)S(1)} %get-tuple-element.7), custom_call_target="InvertDiagBlocksLowerTriangular" | custom-call | tf_op jit(solution)/shard_map/jit(cholesky)/cholesky | solution.py:13
  260.7 11.7 %custom-call.33 = f32[1,128,128]{2,1,0:T(8,128)S(1)} custom-call(f32[1,128,128]{2,1,0:T(8,128)S(1)} %cholesky.268), custom_call_target="Cholesky" | custom-call | tf_op jit(solution)/shard_map/jit(cholesky)/cholesky | solution.py:13
  274.8 10.8 %custom-call.34 = f32[1,1,128,128]{2,3,1,0:T(8,128)S(1)} custom-call(f32[1,1,128,128]{3,2,1,0:T(8,128)} %get-tuple-element.5), custom_call_target="InvertDiagBlocksLowerTriangular" | custom-call | tf_op jit(solution)/shard_map/jit(cholesky)/cholesky | solution.py:13
  286.7 1.5 fusion.4
  288.3 11.7 %custom-call.35 = f32[1,128,128]{2,1,0:T(8,128)S(1)} custom-call(f32[1,128,128]{2,1,0:T(8,128)S(1)} %cholesky.273), custom_call_target="Cholesky" | custom-call | tf_op jit(solution)/shard_map/jit(cholesky)/cholesky | solution.py:13
  300.1 9.8 %custom-call.36 = f32[1,1,128,128]{2,3,1,0:T(8,128)S(1)} custom-call(f32[1,1,128,128]{3,2,1,0:T(8,128)S(1)} %get-tuple-element.3), custom_call_target="InvertDiagBlocksLowerTriangular" | custom-call | tf_op jit(solution)/shard_map/jit(cholesky)/cholesky | solution.py:13
  310.2 1.3 fusion.6
  311.6 11.7 %custom-call.37 = f32[1,128,128]{2,1,0:T(8,128)S(1)} custom-call(f32[1,128,128]{2,1,0:T(8,128)S(1)} %fusion.6), custom_call_target="Cholesky" | custom-call | tf_op jit(solution)/shard_map/jit(cholesky)/cholesky | solution.py:13
  (46 shorter events, 17.5 us)
Async XLA Ops:
  7.2 93.0 %copy-start = (bf16[128,128,64]{1,2,0:T(8,128)(2,1)S(1)}, bf16[128,128,64]{1,2,0:T(8,128)(2,1)}, u32[]{:S(2)}) copy-start(bf16[128,128,64]{1,2,0:T(8,128)(2,1)} %param.9) | copy-start | bytes 6291460
  11.5 27.0 %all-to-all-start = ((bf16[8,32,1024]{2,1,0:T(8,128)(2,1)}), bf16[8,32,1024]{2,1,0:T(8,128)(2,1)S(1)}, u32[]{:S(2)}, u32[]{:S(2)}) async-start(bf16[8,32,1024]{2,1,0:T(8,128)(2,1)} %bitcast.2), calls=%async_computation | async-start | bytes 1048576 | tf_op jit(solution)/shard_map/all_to_all | solution.py:23
  38.4 4.5 %copy-start.2 = (s32[128]{0:T(128)S(1)}, s32[128]{0:T(128)}, u32[]{:S(2)}) copy-start(s32[128]{0:T(128)} %param.10) | copy-start | bytes 1540
  38.4 47.6 %all-to-all-start.1 = ((bf16[8,32,3584]{2,1,0:T(8,128)(2,1)}), bf16[8,32,3584]{2,1,0:T(8,128)(2,1)}, u32[]{:S(2)}, u32[]{:S(2)}) async-start(bf16[8,32,3584]{2,1,0:T(8,128)(2,1)} %bitcast.97), calls=%async_computation.1 | async-start | bytes 3670016 | tf_op jit(solution)/shard_map/all_to_all | solution.py:24
  42.9 187.0 %all-reduce.3.cloned.1.call-start = ((), (), s32[]{:S(2)}) async-start(), calls=%async_computation.3 | async-start | bytes 1048576 | tf_op jit(solution)/shard_map/psum | solution.py:43
  234.8 1.0 copy-start.1
Sparse Core Ops, SparseCore 0:
  116.8 112.9 all-reduce.2
where the time goes:
time: 337 us; the launch traced here: 336 us
  waiting for transfers between devices  165 us (49%)
  other arithmetic  85.7 us (25%)
  local copies, waits for them, and re-layouts  31.8 us (9%)
  between operations  16.8 us (5%)
  blocking collectives  13.9 us (4%)
  starting transfers between devices  13.5 us (4%)
  matrix products  9.39 us (3%)
    psum x1, waiting for transfers between devices, shards(): lax.psum(gram_blocks.astype(jnp.bfloat16), 'dp').astype(jnp.float32)  112 us
    another operation x14, other arithmetic, upper_factor(): return jnp.swapaxes(jnp.linalg.cholesky(matrix), 1, 2)  80 us
    all_to_all x1, waiting for transfers between devices, shards(): lax.all_to_all(grads[row_order], 'mp', split_axis=0, concat_axis=1, tiled...  41.4 us
    all_to_all x1, blocking collectives, shards(): lax.all_to_all(features, 'mp', split_axis=1, concat_axis=0, tiled=True)  13.9 us
    all_to_all x1, waiting for transfers between devices, shards(): lax.all_to_all(acts[row_order], 'mp', split_axis=0, concat_axis=1, tiled=...  11.5 us
    all_to_all x1, starting transfers between devices, shards(): lax.all_to_all(acts[row_order], 'mp', split_axis=0, concat_axis=1, tiled=...  9 us
    reshape x2, local copies, waits for them, and re-layouts, shards(): grid = moved_grads.reshape(ex_rows, -1, block_rows)  8.13 us
  transfers between devices with their start and end apart: 3, of which 3 were waited for; matrix products, arithmetic and copies ran while one was open for 3% of the time, Pallas kernels for 0%

commit v1 on v0

v1 whole, which is shorter than its diff:
```python
import functools

import jax
import jax.numpy as jnp
from jax import lax
from jax.experimental import pallas as pl
from jax.experimental.pallas import tpu as pltpu
from jax.sharding import PartitionSpec as P

FB = 512
DAMPING = 0.05
BF16 = jnp.bfloat16
F32 = jnp.float32
NT = (((1,), (1,)), ((), ()))


def nt_dot(a, b):
    return lax.dot_general(a, b, NT, preferred_element_type=F32)


def project_kernel(index_ref, assign_ref, acts_hbm, grads_hbm, proj_hbm, vals_hbm, send_ref,
                   acts, grads, proj, vals, flags, sems, val_sems):
    me = lax.axis_index("mp")
    k_in = acts.shape[1]
    blocks = val_sems.shape[0]
    copies = (
        pltpu.make_async_copy(proj_hbm.at[:, pl.ds(pl.multiple_of(me * k_in, 128), k_in)], proj, sems.at[0]),
        pltpu.make_async_copy(acts_hbm, acts, sems.at[1]),
        pltpu.make_async_copy(grads_hbm, grads, sems.at[2]),
    )
    for copy in copies:
        copy.start()

    def clear(j, carry):
        flags[j] = -1
        return carry

    lax.fori_loop(0, blocks, clear, 0)

    def value_copy(j, t):
        return pltpu.make_async_copy(
            vals_hbm.at[t], vals.at[:, pl.ds(pl.multiple_of(j * 128, 128), 128)], val_sems.at[j])

    def find(t, carry):
        j = index_ref[t] - me * blocks

        @pl.when((j >= 0) & (j < blocks))
        def _():
            flags[j] = t
            value_copy(j, t).start()

        return carry

    lax.fori_loop(0, index_ref.shape[0], find, 0)

    def blank(j, carry):
        @pl.when(flags[j] < 0)
        def _():
            vals[:, pl.ds(pl.multiple_of(j * 128, 128), 128)] = jnp.zeros((vals.shape[0], 128), BF16)

        return carry

    lax.fori_loop(0, blocks, blank, 0)

    examples = acts.shape[0]
    rows = lax.broadcasted_iota(jnp.int32, (examples, examples), 0)
    order = jnp.where(rows == assign_ref[...], 1.0, 0.0).astype(BF16)
    copies[0].wait()
    copies[1].wait()
    in_part = nt_dot(proj[...], acts[...]).astype(BF16)
    in_part = jnp.dot(in_part, order, preferred_element_type=F32)

    def settle(j, carry):
        @pl.when(flags[j] >= 0)
        def _():
            value_copy(j, flags[j]).wait()

        return carry

    lax.fori_loop(0, blocks, settle, 0)
    copies[2].wait()
    out_part = nt_dot(vals[...], grads[...]).astype(BF16)
    out_part = jnp.dot(out_part, order, preferred_element_type=F32)
    for c in range(send_ref.shape[0]):
        send_ref[c, 0:64, :] = out_part[:, 0:128].astype(BF16)
        send_ref[c, 64:128, :] = out_part[:, 128:256].astype(BF16)
        tops = jnp.concatenate([in_part[8 * c:8 * c + 8, 0:128], in_part[8 * c:8 * c + 8, 128:256]], axis=0)
        send_ref[c, 128:144, :] = tops.astype(BF16)
        mine = jnp.concatenate(
            [in_part[16 * k:16 * k + 16, 32 * c:32 * c + 32] for k in range(4)], axis=1)
        send_ref[c, 144:160, :] = mine.astype(BF16)


TILES = [(i, j) for i in range(4) for j in range(i, 4)]


def gram_kernel(recv_ref, coords_ref, keep_ref, give_ref, ft, packed):
    total = recv_ref[0].astype(F32)
    for c in range(1, recv_ref.shape[0]):
        total = total + recv_ref[c].astype(F32)
    coords = total.astype(BF16)
    coords_ref[...] = coords
    wide = coords.astype(F32)
    out_t = (wide[0:64], wide[64:128])
    in_t = (wide[128:136], wide[136:144])
    for p in range(8):
        for h in range(2):
            ft[64 * p:64 * p + 64, 128 * h:128 * h + 128] = (in_t[h][p:p + 1] * out_t[h]).astype(BF16)
    for at, (i, j) in enumerate(TILES):
        packed[128 * at:128 * at + 128, :] = nt_dot(
            ft[128 * i:128 * i + 128, :], ft[128 * j:128 * j + 128, :]).astype(BF16)
    core = lax.rem(lax.axis_index("dp"), 2)
    half = packed.shape[0] // 2
    keep_ref[...] = packed[pl.ds(pl.multiple_of(core * half, half), half), :]
    give_ref[...] = packed[pl.ds(pl.multiple_of((1 - core) * half, half), half), :]


def features_kernel(coords_ref, features_ref):
    me = lax.axis_index("mp")
    coords = coords_ref[...]
    picked = jnp.concatenate([coords[0:64], coords[64:128]], axis=1)
    rows = lax.broadcasted_iota(jnp.int32, (32, 256), 0)
    cols = lax.broadcasted_iota(jnp.int32, (32, 256), 1)
    pick = jnp.where(cols == rows + 32 * me, 1.0, 0.0).astype(BF16)
    outs = nt_dot(pick, picked)
    wide = coords[144:160].astype(F32)
    mine = jnp.concatenate([wide[:, 32 * k:32 * k + 32] for k in range(4)], axis=0).astype(BF16)
    turn = jnp.where(
        lax.broadcasted_iota(jnp.int32, (32, 32), 0) == lax.broadcasted_iota(jnp.int32, (32, 32), 1),
        1.0, 0.0).astype(BF16)
    ins = nt_dot(turn, mine).astype(BF16)
    both = jnp.concatenate([outs, outs], axis=1)
    step = 512
    for at in range(features_ref.shape[1] // step):
        p = lax.broadcasted_iota(jnp.int32, (64, step), 0)
        f = lax.broadcasted_iota(jnp.int32, (64, step), 1)
        spread = jnp.where(p == (step // 64) * at + lax.div(f, 64), 1.0, 0.0).astype(BF16)
        left = jnp.dot(ins, spread, preferred_element_type=F32)
        for w in range(step // 128):
            features_ref[:, step * at + 128 * w:step * at + 128 * w + 128] = (
                left[:, 128 * w:128 * w + 128] * both).astype(BF16)


def spot(y, x, core):
    return (y * 4 + x) * 2 + core


def moves(step):
    return [(spot(y, x, c), spot(*step(y, x, c)))
            for y in range(4) for x in range(4) for c in range(2)]


def shards(acts, grads, proj_in, block_vals, block_index, assign):
    ex, k_in = acts.shape
    k_out = grads.shape[1]
    any_spec = pl.BlockSpec(memory_space=pl.ANY)
    vmem = pl.BlockSpec(memory_space=pltpu.VMEM)
    smem = pl.BlockSpec(memory_space=pltpu.SMEM)
    send = pl.pallas_call(
        project_kernel,
        out_shape=jax.ShapeDtypeStruct((8, 160, 128), BF16),
        in_specs=[smem, vmem, any_spec, any_spec, any_spec, any_spec],
        out_specs=vmem,
        scratch_shapes=[
            pltpu.VMEM((ex, k_in), BF16),
            pltpu.VMEM((ex, k_out), BF16),
            pltpu.VMEM((64, k_in), BF16),
            pltpu.VMEM((64, k_out), BF16),
            pltpu.SMEM((k_out // 128,), jnp.int32),
            pltpu.SemaphoreType.DMA((3,)),
            pltpu.SemaphoreType.DMA((k_out // 128,)),
        ],
        name="project",
    )(block_index, assign, acts, grads, proj_in.T, jnp.swapaxes(block_vals, 1, 2))
    recv = lax.all_to_all(send, "mp", 0, 0, tiled=True)
    coords, keep, give = pl.pallas_call(
        gram_kernel,
        out_shape=(
            jax.ShapeDtypeStruct((160, 128), BF16),
            jax.ShapeDtypeStruct((640, 128), BF16),
            jax.ShapeDtypeStruct((640, 128), BF16),
        ),
        in_specs=[vmem],
        out_specs=(vmem, vmem, vmem),
        scratch_shapes=[pltpu.VMEM((FB, 256), BF16), pltpu.VMEM((1280, 128), BF16)],
        name="gram",
    )(recv)
    features = pl.pallas_call(
        features_kernel,
        out_shape=jax.ShapeDtypeStruct((32, 4096), BF16),
        in_specs=[vmem],
        out_specs=vmem,
        cost_estimate=pl.CostEstimate(flops=2 * 32 * 64 * 4096, bytes_accessed=300000, transcendentals=0),
        name="features",
    )(coords)
    total = keep + lax.ppermute(give, "dp", moves(lambda y, x, c: (y, x, 1 - c)))
    for step in (
        lambda y, x, c: (y, x ^ 1, c),
        lambda y, x, c: (y, 3 - x, c),
        lambda y, x, c: (y ^ 1, x, c),
        lambda y, x, c: (3 - y, x, c),
    ):
        total = total + lax.ppermute(total, "dp", moves(step))
    other = lax.ppermute(total, "dp", moves(lambda y, x, c: (y, x, 1 - c)))
    core = lax.rem(lax.axis_index("dp"), 2)
    packed = jnp.where(core == 0, jnp.concatenate([total, other]), jnp.concatenate([other, total]))
    tiles = packed.reshape(10, 128, 128).astype(F32)
    grid = {}
    for at, (i, j) in enumerate(TILES):
        grid[i, j] = tiles[at]
        if i != j:
            grid[j, i] = tiles[at].T
    gram = jnp.concatenate([jnp.concatenate([grid[i, j] for j in range(4)], axis=1) for i in range(4)])
    cov = gram / 8192 + DAMPING * jnp.eye(FB, dtype=F32)
    factor = jnp.swapaxes(jnp.linalg.cholesky(cov[None]), 1, 2)
    return features, factor


def solution(mesh):
    return jax.shard_map(
        shards,
        mesh=mesh,
        in_specs=(P("dp", "mp"), P("dp", "mp"), P(), P(), P(), P("dp", None)),
        out_specs=(P(("dp", "mp"), None), P("mp", None, None)),
        check_vma=False,
    )
```

time: 337 us -> 150 us (0.45)
  waiting for transfers between devices: 165 us -> 13.1 us
  local copies, waits for them, and re-layouts: 31.8 us -> 3.91 us
  between operations: 16.8 us -> 3.49 us
  Pallas kernels: 0 us -> 9.6 us
  matrix products: 9.39 us -> 2.31 us
  blocking collectives: 13.9 us -> 20.8 us
  other arithmetic: 85.7 us -> 81 us
    psum x1 -> x0, waiting for transfers between devices: 112 us -> none  [shards(): lax.psum(gram_blocks.astype(jnp.bfloat16), 'dp').astype(jnp.float32)]
    all_to_all x2 -> x0, waiting for transfers between devices: 52.9 us -> none  [the longest x1 41.4 us: shards(): lax.all_to_all(grads[row_order], 'mp', split_axis=0, concat_axis=1, tiled...]
    ppermute x0 -> x6, starting transfers between devices: none -> 15.2 us  [the longest x4 8.07 us: shards(): total = total + lax.ppermute(total, 'dp', moves(step))]
    all_to_all x2 -> x0, starting transfers between devices: 13.4 us -> none  [the longest x1 9 us: shards(): lax.all_to_all(acts[row_order], 'mp', split_axis=0, concat_axis=1, tiled=...]
    ppermute x0 -> x6, waiting for transfers between devices: none -> 13.1 us  [the longest x4 13.1 us: shards(): total = total + lax.ppermute(total, 'dp', moves(step))]
    gather x3 -> x0, local copies, waits for them, and re-layouts: 12.2 us -> none  [the longest x1 6.49 us: shards(): grads[row_order]]
    pallas_call x0 -> x3, Pallas kernels: none -> 9.6 us  [the longest x1 5.57 us: shards(): pl.pallas_call(project_kernel, out_shape=jax.ShapeDtypeStruct((8, 160, 12...]
    reshape x2 -> x0, local copies, waits for them, and re-layouts: 8.13 us -> none  [shards(): grid = moved_grads.reshape(ex_rows, -1, block_rows)]
  transfers between devices with their start and end apart: 3 -> 6, of which waited for: 3 -> 4; matrix products, arithmetic and copies ran while one was open for 3% -> 1% of each run, Pallas kernels for 0% -> 1%
where the time goes in v1:
time: 150 us; the launch traced here: 149 us
  other arithmetic  81 us (54%)
  blocking collectives  20.8 us (14%)
  starting transfers between devices  15.2 us (10%)
  waiting for transfers between devices  13.1 us (9%)
  Pallas kernels  9.6 us (6%)
  local copies, waits for them, and re-layouts  3.91 us (3%)
  between operations  3.49 us (2%)
  matrix products  2.31 us (2%)
    another operation x15, other arithmetic, shards(): factor = jnp.swapaxes(jnp.linalg.cholesky(cov[None]), 1, 2)  79.2 us
    all_to_all x1, blocking collectives, shards(): recv = lax.all_to_all(send, 'mp', 0, 0, tiled=True)  20.8 us
    ppermute x4, waiting for transfers between devices, shards(): total = total + lax.ppermute(total, 'dp', moves(step))  13.1 us
    ppermute x4, starting transfers between devices, shards(): total = total + lax.ppermute(total, 'dp', moves(step))  8.07 us
    pallas_call x1, Pallas kernels, shards(): pl.pallas_call(project_kernel, out_shape=jax.ShapeDtypeStruct((8, 160, 12...  5.57 us
    ppermute x1, starting transfers between devices, shards(): other = lax.ppermute(total, 'dp', moves(lambda y, x, c: (y, x, 1 - c)))  4.52 us
  transfers between devices with their start and end apart: 6, of which 4 were waited for; matrix products, arithmetic and copies ran while one was open for 1% of the time, Pallas kernels for 1%

profile of v1, /device:TPU:1, one launch (start us, length us, event | category | flops | bytes accessed | tf_op | source)
XLA Modules:
  0.0 149.5 jit_solution(12394627675368316205)
XLA Ops:
  0.6 5.6 %project.1 = bf16[8,160,128]{2,1,0:T(8,128)(2,1)} custom-call(s32[128]{0:T(128)} %index_ref.1, s32[1,256]{1,0:T(1,128)} %assign_ref.1, bf16[256,1024]{1,0:T(8,128)(2,1)} %acts_hbm.1, bf16[256,3584]{1,0:T(8,128)(2,1)} %grads_hbm.1, bf16[64,8192]{1,0:T(8,128)(2,1)} %bitcast.87, bf16[128,64,128]{2,1,0:T(8,128)(2,1)} %bitcast.85), custom_call_target="tpu_custom_call" | custom-call | tf_op jit(solution)/shard_map/project/pallas_call | solution.py:159
  6.2 20.8 %all_to_all.5.recv_ref = bf16[8,160,128]{2,1,0:T(8,128)(2,1)} all-to-all(bf16[8,160,128]{2,1,0:T(8,128)(2,1)} %project.1), channel_id=1, replica_groups=mesh['dp'=32,'mp'=8] {'mp'}, dimensions={0} | all-to-all | bytes 655360 | tf_op jit(solution)/shard_map/all_to_all | solution.py:175
  27.1 2.1 %gram.1 = (bf16[160,128]{1,0:T(8,128)(2,1)}, bf16[640,128]{1,0:T(8,128)(2,1)}, bf16[640,128]{1,0:T(8,128)(2,1)}) custom-call(bf16[8,160,128]{2,1,0:T(8,128)(2,1)} %all_to_all.5.recv_ref), custom_call_target="tpu_custom_call" | custom-call | tf_op jit(solution)/shard_map/gram/pallas_call | solution.py:176
  29.2 1.1 copy.8
  30.3 2.6 %collective-permute-start = (bf16[640,128]{0,1:T(8,128)(2,1)S(1)}, bf16[640,128]{0,1:T(8,128)(2,1)S(1)}, u32[]{:S(2)}, u32[]{:S(2)}) collective-permute-start(bf16[640,128]{0,1:T(8,128)(2,1)S(1)} %copy.8), channel_id=1, source_target_pairs={{0,8},{8,0},{16,24},{24,16},{32,40},{40,32},{48,56},{56,48},{64,72... | collective-permute-start | bytes 491528 | tf_op jit(solution)/shard_map/ppermute | solution.py:196
  32.9 1.1 copy.9
  34.0 1.3 collective-permute-start.1
  35.3 4.2 %collective-permute-done.1 = bf16[640,128]{0,1:T(8,128)(2,1)S(1)} collective-permute-done((bf16[640,128]{0,1:T(8,128)(2,1)S(1)}, bf16[640,128]{0,1:T(8,128)(2,1)S(1)}, u32[]{:S(2)}, u32[]{:S(2)}) %collective-permute-start.1) | collective-permute-done | bytes 163872 | tf_op jit(solution)/shard_map/ppermute | solution.py:203
  39.6 2.6 %collective-permute-start.2 = (bf16[640,128]{0,1:T(8,128)(2,1)S(1)}, bf16[640,128]{0,1:T(8,128)(2,1)S(1)}, u32[]{:S(2)}, u32[]{:S(2)}) collective-permute-start(bf16[640,128]{0,1:T(8,128)(2,1)S(1)} %add.64), channel_id=1, source_target_pairs={{0,48},{8,56},{16,32},{24,40},{32,16},{40,24},{48,0},{56,8},{64,11... | collective-permute-start | bytes 491528 | tf_op jit(solution)/shard_map/ppermute | solution.py:203
  42.1 3.3 %collective-permute-done.2 = bf16[640,128]{0,1:T(8,128)(2,1)S(1)} collective-permute-done((bf16[640,128]{0,1:T(8,128)(2,1)S(1)}, bf16[640,128]{0,1:T(8,128)(2,1)S(1)}, u32[]{:S(2)}, u32[]{:S(2)}) %collective-permute-start.2) | collective-permute-done | bytes 163872 | tf_op jit(solution)/shard_map/ppermute | solution.py:203
  45.5 1.4 collective-permute-start.3
  46.9 2.9 %collective-permute-done.3 = bf16[640,128]{0,1:T(8,128)(2,1)S(1)} collective-permute-done((bf16[640,128]{0,1:T(8,128)(2,1)S(1)}, bf16[640,128]{0,1:T(8,128)(2,1)S(1)}, u32[]{:S(2)}, u32[]{:S(2)}) %collective-permute-start.3) | collective-permute-done | bytes 163872 | tf_op jit(solution)/shard_map/ppermute | solution.py:203
  49.8 2.8 %collective-permute-start.4 = (bf16[640,128]{0,1:T(8,128)(2,1)S(1)}, bf16[640,128]{0,1:T(8,128)(2,1)S(1)}, u32[]{:S(2)}, u32[]{:S(2)}) collective-permute-start(bf16[640,128]{0,1:T(8,128)(2,1)S(1)} %add.66), channel_id=1, source_target_pairs={{0,192},{8,200},{16,208},{24,216},{32,224},{40,232},{48,240},{56,2... | collective-permute-start | bytes 491528 | tf_op jit(solution)/shard_map/ppermute | solution.py:203
  52.6 2.7 %collective-permute-done.4 = bf16[640,128]{0,1:T(8,128)(2,1)S(1)} collective-permute-done((bf16[640,128]{0,1:T(8,128)(2,1)S(1)}, bf16[640,128]{0,1:T(8,128)(2,1)S(1)}, u32[]{:S(2)}, u32[]{:S(2)}) %collective-permute-start.4) | collective-permute-done | bytes 163872 | tf_op jit(solution)/shard_map/ppermute | solution.py:203
  55.4 4.5 %collective-permute-start.5 = (bf16[640,128]{0,1:T(8,128)(2,1)S(1)}, bf16[640,128]{0,1:T(8,128)(2,1)S(1)}, u32[]{:S(2)}, u32[]{:S(2)}) collective-permute-start(bf16[640,128]{0,1:T(8,128)(2,1)S(1)} %add.67), channel_id=1, source_target_pairs={{0,8},{8,0},{16,24},{24,16},{32,40},{40,32},{48,56},{56,48},{64,72... | collective-permute-start | bytes 491528 | tf_op jit(solution)/shard_map/ppermute | solution.py:204
  59.9 1.9 %features.1 = bf16[32,4096]{1,0:T(8,128)(2,1)} custom-call(bf16[160,128]{1,0:T(8,128)(2,1)} %get-tuple-element.5.coords_ref), custom_call_target="tpu_custom_call" | custom-call | flops 16777216 | bytes 300000 | tf_op jit(solution)/shard_map/features/pallas_call | solution.py:188
  63.5 11.7 %custom-call.31 = f32[1,128,128]{2,1,0:T(8,128)S(1)} custom-call(f32[1,128,128]{2,1,0:T(8,128)S(1)} %cholesky.264), custom_call_target="Cholesky" | custom-call | tf_op jit(solution)/shard_map/jit(cholesky)/cholesky | solution.py:215
  75.3 9.8 %custom-call.32 = f32[1,1,128,128]{2,3,1,0:T(8,128)S(1)} custom-call(f32[1,1,128,128]{3,2,1,0:T(8,128)S(1)} %get-tuple-element.27), custom_call_target="InvertDiagBlocksLowerTriangular" | custom-call | tf_op jit(solution)/shard_map/jit(cholesky)/cholesky | solution.py:215
  85.9 11.7 %custom-call.33 = f32[1,128,128]{2,1,0:T(8,128)S(1)} custom-call(f32[1,128,128]{2,1,0:T(8,128)S(1)} %cholesky.268), custom_call_target="Cholesky" | custom-call | tf_op jit(solution)/shard_map/jit(cholesky)/cholesky | solution.py:215
  98.0 10.0 %custom-call.34 = f32[1,1,128,128]{2,3,1,0:T(8,128)S(1)} custom-call(f32[1,1,128,128]{3,2,1,0:T(8,128)S(1)} %get-tuple-element.25), custom_call_target="InvertDiagBlocksLowerTriangular" | custom-call | tf_op jit(solution)/shard_map/jit(cholesky)/cholesky | solution.py:215
  108.9 11.7 %custom-call.35 = f32[1,128,128]{2,1,0:T(8,128)S(1)} custom-call(f32[1,128,128]{2,1,0:T(8,128)S(1)} %cholesky.273), custom_call_target="Cholesky" | custom-call | tf_op jit(solution)/shard_map/jit(cholesky)/cholesky | solution.py:215
  120.7 9.8 %custom-call.36 = f32[1,1,128,128]{2,3,1,0:T(8,128)S(1)} custom-call(f32[1,1,128,128]{3,2,1,0:T(8,128)S(1)} %get-tuple-element.23), custom_call_target="InvertDiagBlocksLowerTriangular" | custom-call | tf_op jit(solution)/shard_map/jit(cholesky)/cholesky | solution.py:215
  131.3 11.7 %custom-call.37 = f32[1,128,128]{2,1,0:T(8,128)S(1)} custom-call(f32[1,128,128]{2,1,0:T(8,128)S(1)} %fusion.4), custom_call_target="Cholesky" | custom-call | tf_op jit(solution)/shard_map/jit(cholesky)/cholesky | solution.py:215
  148.4 1.1 select_bitcast_fusion
  (49 shorter events, 7.6 us)
Async XLA Ops:
  30.3 3.6 %collective-permute-start = (bf16[640,128]{0,1:T(8,128)(2,1)S(1)}, bf16[640,128]{0,1:T(8,128)(2,1)S(1)}, u32[]{:S(2)}, u32[]{:S(2)}) collective-permute-start(bf16[640,128]{0,1:T(8,128)(2,1)S(1)} %copy.8), channel_id=1, source_target_pairs={{0,8},{8,0},{16,24},{24,16},{32,40},{40,32},{48,56},{56,48},{64,72... | collective-permute-start | bytes 491528 | tf_op jit(solution)/shard_map/ppermute | solution.py:196
  34.0 5.5 %collective-permute-start.1 = (bf16[640,128]{0,1:T(8,128)(2,1)S(1)}, bf16[640,128]{0,1:T(8,128)(2,1)S(1)}, u32[]{:S(2)}, u32[]{:S(2)}) collective-permute-start(bf16[640,128]{0,1:T(8,128)(2,1)S(1)} %add.63), channel_id=1, source_target_pairs={{0,16},{8,24},{16,0},{24,8},{32,48},{40,56},{48,32},{56,40},{64,80... | collective-permute-start | bytes 491528 | tf_op jit(solution)/shard_map/ppermute | solution.py:203
  39.6 5.9 %collective-permute-start.2 = (bf16[640,128]{0,1:T(8,128)(2,1)S(1)}, bf16[640,128]{0,1:T(8,128)(2,1)S(1)}, u32[]{:S(2)}, u32[]{:S(2)}) collective-permute-start(bf16[640,128]{0,1:T(8,128)(2,1)S(1)} %add.64), channel_id=1, source_target_pairs={{0,48},{8,56},{16,32},{24,40},{32,16},{40,24},{48,0},{56,8},{64,11... | collective-permute-start | bytes 491528 | tf_op jit(solution)/shard_map/ppermute | solution.py:203
  45.5 4.3 %collective-permute-start.3 = (bf16[640,128]{0,1:T(8,128)(2,1)S(1)}, bf16[640,128]{0,1:T(8,128)(2,1)S(1)}, u32[]{:S(2)}, u32[]{:S(2)}) collective-permute-start(bf16[640,128]{0,1:T(8,128)(2,1)S(1)} %add.65), channel_id=1, source_target_pairs={{0,64},{8,72},{16,80},{24,88},{32,96},{40,104},{48,112},{56,120},{... | collective-permute-start | bytes 491528 | tf_op jit(solution)/shard_map/ppermute | solution.py:203
  49.8 5.5 %collective-permute-start.4 = (bf16[640,128]{0,1:T(8,128)(2,1)S(1)}, bf16[640,128]{0,1:T(8,128)(2,1)S(1)}, u32[]{:S(2)}, u32[]{:S(2)}) collective-permute-start(bf16[640,128]{0,1:T(8,128)(2,1)S(1)} %add.66), channel_id=1, source_target_pairs={{0,192},{8,200},{16,208},{24,216},{32,224},{40,232},{48,240},{56,2... | collective-permute-start | bytes 491528 | tf_op jit(solution)/shard_map/ppermute | solution.py:203
  55.4 6.4 %collective-permute-start.5 = (bf16[640,128]{0,1:T(8,128)(2,1)S(1)}, bf16[640,128]{0,1:T(8,128)(2,1)S(1)}, u32[]{:S(2)}, u32[]{:S(2)}) collective-permute-start(bf16[640,128]{0,1:T(8,128)(2,1)S(1)} %add.67), channel_id=1, source_target_pairs={{0,8},{8,0},{16,24},{24,16},{32,40},{40,32},{48,56},{56,48},{64,72... | collective-permute-start | bytes 491528 | tf_op jit(solution)/shard_map/ppermute | solution.py:204

commit v2 on v1

--- a/solution.py
+++ b/solution.py
@@ -140,6 +140,77 @@
             features_ref[:, step * at + 128 * w:step * at + 128 * w + 128] = (
                 left[:, 128 * w:128 * w + 128] * both).astype(BF16)
 
+
+def spread_lane(x, at):
+    return jnp.take_along_axis(x, jnp.full((8, 128), at, jnp.int32), axis=1)
+
+def row(x, j):
+    return jnp.broadcast_to(x[j:j + 1, :], (8, 128))
+
+def factor_block(c):
+    sub = lax.broadcasted_iota(jnp.int32, (8, 128), 0)
+    lane = lax.broadcasted_iota(jnp.int32, (8, 128), 1)
+    n = len(c)
+    upper, inverse = [], []
+    for p in range(n):
+        base = 8 * p
+        inside = (lane >= base) & (lane < base + 8)
+        cols = [spread_lane(c[p], base + k) for k in range(8)]
+        own = c[p]
+        aug = jnp.where(inside, jnp.where(lane - base == sub, 1.0, 0.0), c[p])
+        zed = aug
+        below = {t: [spread_lane(c[t], base + k) for k in range(8)] for t in range(p + 1, n)}
+        inv = jnp.zeros((8, 128), F32)
+        for j in range(8):
+            r = 1.0 / row(cols[j], j)
+            inv = jnp.where(sub == j, r, inv)
+            full = jnp.where(sub == j, 0.0, cols[j])
+            part = jnp.where(sub > j, cols[j], 0.0)
+            for k in range(j + 1, 8):
+                cols[k] = cols[k] - (full * row(cols[k], j)) * r
+            ro, ra, rz = row(own, j), row(aug, j), row(zed, j)
+            own = own - (part * ro) * r
+            aug = aug - (part * ra) * r
+            zed = zed - (full * rz) * r
+        zed = zed * inv
+        root = jnp.sqrt(inv)
+        upper.append(jnp.where(lane >= base + sub, own * root, 0.0))
+        inverse.append(jnp.where(lane <= base + sub, aug * root, 0.0))
+        rows = [row(zed, k) for k in range(8)]
+        for t in range(p + 1, n):
+            s = [below[t][k] * rows[k] for k in range(8)]
+            s = ((s[0] + s[1]) + (s[2] + s[3])) + ((s[4] + s[5]) + (s[6] + s[7]))
+            c[t] = jnp.where(inside, 0.0, c[t]) - s
+    return upper, inverse
+
+def factor_kernel(total_ref, other_ref, out_ref, work, inv):
+    core = lax.rem(lax.axis_index("dp"), 2)
+    half = total_ref.shape[0]
+    at0 = pl.multiple_of(core * half, half); at1 = pl.multiple_of((1 - core) * half, half)
+    work[pl.ds(at0, half), :] = total_ref[...].astype(F32) * (1.0 / 8192)
+    work[pl.ds(at1, half), :] = other_ref[...].astype(F32) * (1.0 / 8192)
+    place = {ij: 128 * n for n, ij in enumerate(TILES)}
+    sub = lax.broadcasted_iota(jnp.int32, (8, 128), 0)
+    lane = lax.broadcasted_iota(jnp.int32, (8, 128), 1)
+    for s in range(4):
+        o = place[s, s]
+        c = [work[o + 8 * t:o + 8 * t + 8, :] + jnp.where(lane == sub + 8 * t, DAMPING, 0.0) for t in range(16)]
+        upper, inverse = factor_block(c)
+        for t in range(16):
+            out_ref[128 * s + 8 * t:128 * s + 8 * t + 8, 128 * s:128 * s + 128] = upper[t]
+            inv[8 * t:8 * t + 8, :] = inverse[t]
+        for j in range(s):
+            out_ref[128 * s:128 * s + 128, 128 * j:128 * j + 128] = jnp.zeros((128, 128), F32)
+        for j in range(s + 1, 4):
+            a = work[place[s, j]:place[s, j] + 128, :]
+            out_ref[128 * s:128 * s + 128, 128 * j:128 * j + 128] = jnp.dot(
+                inv[...], a, preferred_element_type=F32, precision=lax.Precision.HIGHEST)
+        for i in range(s + 1, 4):
+            for j in range(i, 4):
+                ri = out_ref[128 * s:128 * s + 128, 128 * i:128 * i + 128]
+                rj = out_ref[128 * s:128 * s + 128, 128 * j:128 * j + 128]
+                work[place[i, j]:place[i, j] + 128, :] -= lax.dot_general(
+                    ri, rj, (((0,), (0,)), ((), ())), preferred_element_type=F32, precision=lax.Precision.HIGHEST)
 
 def spot(y, x, core):
     return (y * 4 + x) * 2 + core
@@ -201,18 +272,16 @@
         lambda y, x, c: (3 - y, x, c),
     ):
         total = total + lax.ppermute(total, "dp", moves(step))
+        total, features = lax.optimization_barrier((total, features))
     other = lax.ppermute(total, "dp", moves(lambda y, x, c: (y, x, 1 - c)))
-    core = lax.rem(lax.axis_index("dp"), 2)
-    packed = jnp.where(core == 0, jnp.concatenate([total, other]), jnp.concatenate([other, total]))
-    tiles = packed.reshape(10, 128, 128).astype(F32)
-    grid = {}
-    for at, (i, j) in enumerate(TILES):
-        grid[i, j] = tiles[at]
-        if i != j:
-            grid[j, i] = tiles[at].T
-    gram = jnp.concatenate([jnp.concatenate([grid[i, j] for j in range(4)], axis=1) for i in range(4)])
-    cov = gram / 8192 + DAMPING * jnp.eye(FB, dtype=F32)
-    factor = jnp.swapaxes(jnp.linalg.cholesky(cov[None]), 1, 2)
+    factor = pl.pallas_call(
+        factor_kernel,
+        out_shape=jax.ShapeDtypeStruct((FB, FB), F32),
+        in_specs=[vmem, vmem],
+        out_specs=vmem,
+        scratch_shapes=[pltpu.VMEM((1280, 128), F32), pltpu.VMEM((128, 128), F32)],
+        name="factor",
+    )(total, other).reshape(1, FB, FB)
     return features, factor
 
 

time: 150 us -> 77.2 us (0.51)
  other arithmetic: 81 us -> 1.15 us
  Pallas kernels: 9.6 us -> 25 us
  local copies, waits for them, and re-layouts: 3.91 us -> 0.67 us
  between operations: 3.49 us -> 0.68 us
  matrix products: 2.31 us -> 0 us
    another operation x15 -> x0, other arithmetic: 79.2 us -> none  [shards(): factor = jnp.swapaxes(jnp.linalg.cholesky(cov[None]), 1, 2)]
    pallas_call x0 -> x1, Pallas kernels: none -> 15.4 us  [shards(): pl.pallas_call(factor_kernel, out_shape=jax.ShapeDtypeStruct((FB, FB), F3...]
    another operation x6 -> x0, matrix products: 2.31 us -> none  [shards(): factor = jnp.swapaxes(jnp.linalg.cholesky(cov[None]), 1, 2)]
    pallas_call x2 -> x0, local copies, waits for them, and re-layouts: 2.13 us -> none  [shards(): pl.pallas_call(gram_kernel, out_shape=(jax.ShapeDtypeStruct((160, 128), B...]
    ppermute x4, waiting for transfers between devices: 13.1 us -> 11.1 us  [shards(): total = total + lax.ppermute(total, 'dp', moves(step))]
  transfers between devices with their start and end apart: 6 -> 6, of which waited for: 4 -> 6; matrix products, arithmetic and copies ran while one was open for 1% -> 0% of each run, Pallas kernels for 1% -> 2%
where the time goes in v2:
time: 77.2 us; the launch traced here: 76.9 us
  Pallas kernels  25 us (32%)
  blocking collectives  20.8 us (27%)
  starting transfers between devices  15.2 us (20%)
  waiting for transfers between devices  13.4 us (17%)
  other arithmetic  1.15 us (1%)
    all_to_all x1, blocking collectives, shards(): recv = lax.all_to_all(send, 'mp', 0, 0, tiled=True)  20.8 us
    pallas_call x1, Pallas kernels, shards(): pl.pallas_call(factor_kernel, out_shape=jax.ShapeDtypeStruct((FB, FB), F3...  15.4 us
    ppermute x4, waiting for transfers between devices, shards(): total = total + lax.ppermute(total, 'dp', moves(step))  11.1 us
    ppermute x4, starting transfers between devices, shards(): total = total + lax.ppermute(total, 'dp', moves(step))  8.08 us
    pallas_call x1, Pallas kernels, shards(): pl.pallas_call(project_kernel, out_shape=jax.ShapeDtypeStruct((8, 160, 12...  5.59 us
    ppermute x1, starting transfers between devices, shards(): other = lax.ppermute(total, 'dp', moves(lambda y, x, c: (y, x, 1 - c)))  4.58 us
    ppermute x1, starting transfers between devices, shards(): lax.ppermute(give, 'dp', moves(lambda y, x, c: (y, x, 1 - c)))  2.51 us
    pallas_call x1, Pallas kernels, shards(): pl.pallas_call(gram_kernel, out_shape=(jax.ShapeDtypeStruct((160, 128), B...  2.15 us
  transfers between devices with their start and end apart: 6, of which 6 were waited for; matrix products, arithmetic and copies ran while one was open for 0% of the time, Pallas kernels for 2%

profile of v2, /device:TPU:1, one launch (start us, length us, event | category | flops | bytes accessed | tf_op | source)
XLA Modules:
  0.0 76.9 jit_solution(6055999320188368043)
XLA Ops:
  0.6 5.6 %project.1 = bf16[8,160,128]{2,1,0:T(8,128)(2,1)} custom-call(s32[128]{0:T(128)} %index_ref.1, s32[1,256]{1,0:T(1,128)} %assign_ref.1, bf16[256,1024]{1,0:T(8,128)(2,1)} %acts_hbm.1, bf16[256,3584]{1,0:T(8,128)(2,1)} %grads_hbm.1, bf16[64,8192]{1,0:T(8,128)(2,1)} %bitcast.4, bf16[128,64,128]{2,1,0:T(8,128)(2,1)} %bitcast.3), custom_call_target="tpu_custom_call" | custom-call | tf_op jit(solution)/shard_map/project/pallas_call | solution.py:230
  6.2 20.8 %all_to_all.5.recv_ref = bf16[8,160,128]{2,1,0:T(8,128)(2,1)} all-to-all(bf16[8,160,128]{2,1,0:T(8,128)(2,1)} %project.1), channel_id=1, replica_groups=mesh['dp'=32,'mp'=8] {'mp'}, dimensions={0} | all-to-all | bytes 655360 | tf_op jit(solution)/shard_map/all_to_all | solution.py:246
  27.1 2.1 %gram.1 = (bf16[160,128]{1,0:T(8,128)(2,1)}, bf16[640,128]{1,0:T(8,128)(2,1)}, bf16[640,128]{1,0:T(8,128)(2,1)}) custom-call(bf16[8,160,128]{2,1,0:T(8,128)(2,1)} %all_to_all.5.recv_ref), custom_call_target="tpu_custom_call" | custom-call | tf_op jit(solution)/shard_map/gram/pallas_call | solution.py:247
  29.2 2.5 %collective-permute-start = (bf16[640,128]{1,0:T(8,128)(2,1)}, bf16[640,128]{1,0:T(8,128)(2,1)S(1)}, u32[]{:S(2)}, u32[]{:S(2)}) collective-permute-start(bf16[640,128]{1,0:T(8,128)(2,1)} %get-tuple-element.14), channel_id=1, source_target_pairs={{0,8},{8,0},{16,24},{24,16},{32,40},{40,32},{48,56},{56,48},{64,72... | collective-permute-start | bytes 491528 | tf_op jit(solution)/shard_map/ppermute | solution.py:267
  31.7 1.2 %collective-permute-done = bf16[640,128]{1,0:T(8,128)(2,1)S(1)} collective-permute-done((bf16[640,128]{1,0:T(8,128)(2,1)}, bf16[640,128]{1,0:T(8,128)(2,1)S(1)}, u32[]{:S(2)}, u32[]{:S(2)}) %collective-permute-start) | collective-permute-done | bytes 163872 | tf_op jit(solution)/shard_map/ppermute | solution.py:267
  33.0 1.0 %add.15 = bf16[640,128]{1,0:T(8,128)(2,1)S(1)} add(bf16[640,128]{1,0:T(8,128)(2,1)} %get-tuple-element.13, bf16[640,128]{1,0:T(8,128)(2,1)S(1)} %collective-permute-done) | non-fusion elementwise | flops 81920 | bytes 491520 | tf_op jit(solution)/shard_map/add | solution.py:267
  33.9 1.3 %collective-permute-start.1 = (bf16[640,128]{1,0:T(8,128)(2,1)S(1)}, bf16[640,128]{1,0:T(8,128)(2,1)S(1)}, u32[]{:S(2)}, u32[]{:S(2)}) collective-permute-start(bf16[640,128]{1,0:T(8,128)(2,1)S(1)} %add.15), channel_id=1, source_target_pairs={{0,16},{8,24},{16,0},{24,8},{32,48},{40,56},{48,32},{56,40},{64,80... | collective-permute-start | bytes 491528 | tf_op jit(solution)/shard_map/ppermute | solution.py:274
  35.2 1.9 %features.1 = bf16[32,4096]{1,0:T(8,128)(2,1)} custom-call(bf16[160,128]{1,0:T(8,128)(2,1)} %get-tuple-element.15.coords_ref), custom_call_target="tpu_custom_call" | custom-call | flops 16777216 | bytes 300000 | tf_op jit(solution)/shard_map/features/pallas_call | solution.py:259
  37.1 2.3 %collective-permute-done.1 = bf16[640,128]{1,0:T(8,128)(2,1)S(1)} collective-permute-done((bf16[640,128]{1,0:T(8,128)(2,1)S(1)}, bf16[640,128]{1,0:T(8,128)(2,1)S(1)}, u32[]{:S(2)}, u32[]{:S(2)}) %collective-permute-start.1) | collective-permute-done | bytes 163872 | tf_op jit(solution)/shard_map/ppermute | solution.py:274
  39.5 2.6 %collective-permute-start.2 = (bf16[640,128]{1,0:T(8,128)(2,1)S(1)}, bf16[640,128]{1,0:T(8,128)(2,1)S(1)}, u32[]{:S(2)}, u32[]{:S(2)}) collective-permute-start(bf16[640,128]{1,0:T(8,128)(2,1)S(1)} %add.16), channel_id=1, source_target_pairs={{0,48},{8,56},{16,32},{24,40},{32,16},{40,24},{48,0},{56,8},{64,11... | collective-permute-start | bytes 491528 | tf_op jit(solution)/shard_map/ppermute | solution.py:274
  42.0 3.3 %collective-permute-done.2 = bf16[640,128]{1,0:T(8,128)(2,1)S(1)} collective-permute-done((bf16[640,128]{1,0:T(8,128)(2,1)S(1)}, bf16[640,128]{1,0:T(8,128)(2,1)S(1)}, u32[]{:S(2)}, u32[]{:S(2)}) %collective-permute-start.2) | collective-permute-done | bytes 163872 | tf_op jit(solution)/shard_map/ppermute | solution.py:274
  45.3 1.4 %collective-permute-start.3 = (bf16[640,128]{1,0:T(8,128)(2,1)S(1)}, bf16[640,128]{1,0:T(8,128)(2,1)S(1)}, u32[]{:S(2)}, u32[]{:S(2)}) collective-permute-start(bf16[640,128]{1,0:T(8,128)(2,1)S(1)} %add.17), channel_id=1, source_target_pairs={{0,64},{8,72},{16,80},{24,88},{32,96},{40,104},{48,112},{56,120},{... | collective-permute-start | bytes 491528 | tf_op jit(solution)/shard_map/ppermute | solution.py:274
  46.7 2.9 %collective-permute-done.3 = bf16[640,128]{1,0:T(8,128)(2,1)S(1)} collective-permute-done((bf16[640,128]{1,0:T(8,128)(2,1)S(1)}, bf16[640,128]{1,0:T(8,128)(2,1)S(1)}, u32[]{:S(2)}, u32[]{:S(2)}) %collective-permute-start.3) | collective-permute-done | bytes 163872 | tf_op jit(solution)/shard_map/ppermute | solution.py:274
  49.6 2.8 %collective-permute-start.4 = (bf16[640,128]{1,0:T(8,128)(2,1)S(1)}, bf16[640,128]{1,0:T(8,128)(2,1)S(1)}, u32[]{:S(2)}, u32[]{:S(2)}) collective-permute-start(bf16[640,128]{1,0:T(8,128)(2,1)S(1)} %add.18), channel_id=1, source_target_pairs={{0,192},{8,200},{16,208},{24,216},{32,224},{40,232},{48,240},{56,2... | collective-permute-start | bytes 491528 | tf_op jit(solution)/shard_map/ppermute | solution.py:274
  52.5 2.7 %collective-permute-done.4 = bf16[640,128]{1,0:T(8,128)(2,1)S(1)} collective-permute-done((bf16[640,128]{1,0:T(8,128)(2,1)S(1)}, bf16[640,128]{1,0:T(8,128)(2,1)S(1)}, u32[]{:S(2)}, u32[]{:S(2)}) %collective-permute-start.4) | collective-permute-done | bytes 163872 | tf_op jit(solution)/shard_map/ppermute | solution.py:274
  55.2 0.0 copy-start
  55.2 4.6 %collective-permute-start.5 = (bf16[640,128]{1,0:T(8,128)(2,1)S(1)}, bf16[640,128]{1,0:T(8,128)(2,1)S(1)}, u32[]{:S(2)}, u32[]{:S(2)}) collective-permute-start(bf16[640,128]{1,0:T(8,128)(2,1)S(1)} %add.19.total_ref), channel_id=1, source_target_pairs={{0,8},{8,0},{16,24},{24,16},{32,40},{40,32},{48,56},{56,48},{64,72... | collective-permute-start | bytes 491528 | tf_op jit(solution)/shard_map/ppermute | solution.py:276
  59.8 1.0 %collective-permute-done.5.other_ref = bf16[640,128]{1,0:T(8,128)(2,1)S(1)} collective-permute-done((bf16[640,128]{1,0:T(8,128)(2,1)S(1)}, bf16[640,128]{1,0:T(8,128)(2,1)S(1)}, u32[]{:S(2)}, u32[]{:S(2)}) %collective-permute-start.5) | collective-permute-done | bytes 163872 | tf_op jit(solution)/shard_map/ppermute | solution.py:276
  60.8 0.0 copy-done
  60.9 0.0 copy-start.1
  60.9 0.7 copy-done.1
  61.5 15.4 %factor.1 = f32[512,512]{1,0:T(8,128)} custom-call(bf16[640,128]{1,0:T(8,128)(2,1)} %copy-done, bf16[640,128]{1,0:T(8,128)(2,1)} %copy-done.1), custom_call_target="tpu_custom_call" | custom-call | tf_op jit(solution)/shard_map/factor/pallas_call | solution.py:277
  (4 shorter events, 0.2 us)
Async XLA Ops:
  29.2 3.7 %collective-permute-start = (bf16[640,128]{1,0:T(8,128)(2,1)}, bf16[640,128]{1,0:T(8,128)(2,1)S(1)}, u32[]{:S(2)}, u32[]{:S(2)}) collective-permute-start(bf16[640,128]{1,0:T(8,128)(2,1)} %get-tuple-element.14), channel_id=1, source_target_pairs={{0,8},{8,0},{16,24},{24,16},{32,40},{40,32},{48,56},{56,48},{64,72... | collective-permute-start | bytes 491528 | tf_op jit(solution)/shard_map/ppermute | solution.py:267
  33.9 5.5 %collective-permute-start.1 = (bf16[640,128]{1,0:T(8,128)(2,1)S(1)}, bf16[640,128]{1,0:T(8,128)(2,1)S(1)}, u32[]{:S(2)}, u32[]{:S(2)}) collective-permute-start(bf16[640,128]{1,0:T(8,128)(2,1)S(1)} %add.15), channel_id=1, source_target_pairs={{0,16},{8,24},{16,0},{24,8},{32,48},{40,56},{48,32},{56,40},{64,80... | collective-permute-start | bytes 491528 | tf_op jit(solution)/shard_map/ppermute | solution.py:274
  39.5 5.8 %collective-permute-start.2 = (bf16[640,128]{1,0:T(8,128)(2,1)S(1)}, bf16[640,128]{1,0:T(8,128)(2,1)S(1)}, u32[]{:S(2)}, u32[]{:S(2)}) collective-permute-start(bf16[640,128]{1,0:T(8,128)(2,1)S(1)} %add.16), channel_id=1, source_target_pairs={{0,48},{8,56},{16,32},{24,40},{32,16},{40,24},{48,0},{56,8},{64,11... | collective-permute-start | bytes 491528 | tf_op jit(solution)/shard_map/ppermute | solution.py:274
  45.3 4.3 %collective-permute-start.3 = (bf16[640,128]{1,0:T(8,128)(2,1)S(1)}, bf16[640,128]{1,0:T(8,128)(2,1)S(1)}, u32[]{:S(2)}, u32[]{:S(2)}) collective-permute-start(bf16[640,128]{1,0:T(8,128)(2,1)S(1)} %add.17), channel_id=1, source_target_pairs={{0,64},{8,72},{16,80},{24,88},{32,96},{40,104},{48,112},{56,120},{... | collective-permute-start | bytes 491528 | tf_op jit(solution)/shard_map/ppermute | solution.py:274
  49.6 5.5 %collective-permute-start.4 = (bf16[640,128]{1,0:T(8,128)(2,1)S(1)}, bf16[640,128]{1,0:T(8,128)(2,1)S(1)}, u32[]{:S(2)}, u32[]{:S(2)}) collective-permute-start(bf16[640,128]{1,0:T(8,128)(2,1)S(1)} %add.18), channel_id=1, source_target_pairs={{0,192},{8,200},{16,208},{24,216},{32,224},{40,232},{48,240},{56,2... | collective-permute-start | bytes 491528 | tf_op jit(solution)/shard_map/ppermute | solution.py:274
  55.2 5.6 %copy-start = (bf16[640,128]{1,0:T(8,128)(2,1)}, bf16[640,128]{1,0:T(8,128)(2,1)S(1)}, u32[]{:S(2)}) copy-start(bf16[640,128]{1,0:T(8,128)(2,1)S(1)} %add.19.total_ref) | copy-start | bytes 491524
  55.2 5.6 %collective-permute-start.5 = (bf16[640,128]{1,0:T(8,128)(2,1)S(1)}, bf16[640,128]{1,0:T(8,128)(2,1)S(1)}, u32[]{:S(2)}, u32[]{:S(2)}) collective-permute-start(bf16[640,128]{1,0:T(8,128)(2,1)S(1)} %add.19.total_ref), channel_id=1, source_target_pairs={{0,8},{8,0},{16,24},{24,16},{32,40},{40,32},{48,56},{56,48},{64,72... | collective-permute-start | bytes 491528 | tf_op jit(solution)/shard_map/ppermute | solution.py:276
  60.9 0.7 copy-start.1

commit v3 on v2

--- a/solution.py
+++ b/solution.py
@@ -147,41 +147,73 @@
 def row(x, j):
     return jnp.broadcast_to(x[j:j + 1, :], (8, 128))
 
+WIDE = 16
+
+
 def factor_block(c):
     sub = lax.broadcasted_iota(jnp.int32, (8, 128), 0)
     lane = lax.broadcasted_iota(jnp.int32, (8, 128), 1)
     n = len(c)
+    h = WIDE // 8
     upper, inverse = [], []
-    for p in range(n):
+    for p in range(0, n, h):
         base = 8 * p
-        inside = (lane >= base) & (lane < base + 8)
-        cols = [spread_lane(c[p], base + k) for k in range(8)]
-        own = c[p]
-        aug = jnp.where(inside, jnp.where(lane - base == sub, 1.0, 0.0), c[p])
-        zed = aug
-        below = {t: [spread_lane(c[t], base + k) for k in range(8)] for t in range(p + 1, n)}
-        inv = jnp.zeros((8, 128), F32)
-        for j in range(8):
-            r = 1.0 / row(cols[j], j)
-            inv = jnp.where(sub == j, r, inv)
-            full = jnp.where(sub == j, 0.0, cols[j])
-            part = jnp.where(sub > j, cols[j], 0.0)
-            for k in range(j + 1, 8):
-                cols[k] = cols[k] - (full * row(cols[k], j)) * r
-            ro, ra, rz = row(own, j), row(aug, j), row(zed, j)
-            own = own - (part * ro) * r
-            aug = aug - (part * ra) * r
-            zed = zed - (full * rz) * r
-        zed = zed * inv
-        root = jnp.sqrt(inv)
-        upper.append(jnp.where(lane >= base + sub, own * root, 0.0))
-        inverse.append(jnp.where(lane <= base + sub, aug * root, 0.0))
-        rows = [row(zed, k) for k in range(8)]
-        for t in range(p + 1, n):
-            s = [below[t][k] * rows[k] for k in range(8)]
-            s = ((s[0] + s[1]) + (s[2] + s[3])) + ((s[4] + s[5]) + (s[6] + s[7]))
-            c[t] = jnp.where(inside, 0.0, c[t]) - s
+        inside = (lane >= base) & (lane < base + WIDE)
+        own = [c[p + u] for u in range(h)]
+        cols = [[spread_lane(own[u], base + k) for u in range(h)] for k in range(WIDE)]
+        if p:
+            cols[0][0] = cols[0][0] + 0.0 * (cols[WIDE - 1][h - 1] + cols[WIDE - 2][h - 1])
+        aug = [jnp.where(inside, jnp.where(lane - base == sub + 8 * u, 1.0, 0.0), own[u]) for u in range(h)]
+        zed = list(aug)
+        near = range(p + h, min(p + 2 * h, n))
+        below = {t: [spread_lane(c[t], base + k) for k in range(WIDE)] for t in near}
+        inv = [jnp.zeros((8, 128), F32) for _ in range(h)]
+        for j in range(WIDE):
+            v, i = divmod(j, 8)
+            r = 1.0 / row(cols[j][v], i)
+            inv[v] = jnp.where(sub == i, r, inv[v])
+            full = [jnp.where(sub == i, 0.0, cols[j][u]) if u == v else cols[j][u] for u in range(h)]
+            m = [x * r for x in full]
+            part = jnp.where(sub > i, m[v], 0.0)
+            for k in range(j + 1, WIDE):
+                s = row(cols[k][v], i)
+                for u in range(h):
+                    if k == j + 1:
+                        cols[k][u] = cols[k][u] - (full[u] * s) * r
+                    else:
+                        cols[k][u] = cols[k][u] - m[u] * s
+            ro, ra, rz = row(own[v], i), row(aug[v], i), row(zed[v], i)
+            for u in range(h):
+                if u >= v:
+                    low = part if u == v else m[u]
+                    own[u] = own[u] - low * ro
+                    aug[u] = aug[u] - low * ra
+                zed[u] = zed[u] - m[u] * rz
+        rows, dones = [], []
+        for u in range(h):
+            root = jnp.sqrt(inv[u])
+            at = base + 8 * u
+            upper.append(jnp.where(lane >= at + sub, own[u] * root, 0.0))
+            inverse.append(jnp.where(lane <= at + sub, aug[u] * root, 0.0))
+            done = zed[u] * inv[u]
+            dones.append(done)
+            rows += [row(done, k) for k in range(8)]
+        for t in near:
+            s = [below[t][k] * rows[k] for k in range(WIDE)]
+            while len(s) > 1:
+                s = [s[k] + s[k + 1] for k in range(0, len(s), 2)]
+            c[t] = jnp.where(inside, 0.0, c[t]) - s[0]
+        far = range(p + 2 * h, n)
+        if far:
+            pad = [jnp.zeros((8, 128), F32)] * n
+            for u in range(h):
+                pad[p + u] = dones[u]
+            change = jnp.dot(jnp.concatenate([c[t] for t in far], axis=0), jnp.concatenate(pad, axis=0),
+                             preferred_element_type=F32, precision=lax.Precision.HIGHEST)
+            for at, t in enumerate(far):
+                c[t] = jnp.where(inside, 0.0, c[t]) - change[8 * at:8 * at + 8]
     return upper, inverse
+
 
 def factor_kernel(total_ref, other_ref, out_ref, work, inv):
     core = lax.rem(lax.axis_index("dp"), 2)
@@ -254,6 +286,7 @@
         in_specs=[vmem],
         out_specs=(vmem, vmem, vmem),
         scratch_shapes=[pltpu.VMEM((FB, 256), BF16), pltpu.VMEM((1280, 128), BF16)],
+        compiler_params=pltpu.CompilerParams(vmem_limit_bytes=12 << 20),
         name="gram",
     )(recv)
     features = pl.pallas_call(
@@ -262,6 +295,7 @@
         in_specs=[vmem],
         out_specs=vmem,
         cost_estimate=pl.CostEstimate(flops=2 * 32 * 64 * 4096, bytes_accessed=300000, transcendentals=0),
+        compiler_params=pltpu.CompilerParams(vmem_limit_bytes=12 << 20),
         name="features",
     )(coords)
     total = keep + lax.ppermute(give, "dp", moves(lambda y, x, c: (y, x, 1 - c)))
@@ -280,6 +314,7 @@
         in_specs=[vmem, vmem],
         out_specs=vmem,
         scratch_shapes=[pltpu.VMEM((1280, 128), F32), pltpu.VMEM((128, 128), F32)],
+        compiler_params=pltpu.CompilerParams(vmem_limit_bytes=12 << 20),
         name="factor",
     )(total, other).reshape(1, FB, FB)
     return features, factor

time: 77.2 us -> 69.5 us (0.900)
  Pallas kernels: 25 us -> 18.5 us
  other arithmetic: 1.15 us -> 0.23 us
    pallas_call x1, Pallas kernels: 15.4 us -> 11.3 us  [shards(): pl.pallas_call(factor_kernel, out_shape=jax.ShapeDtypeStruct((FB, FB), F3...]
    pallas_call x1, Pallas kernels: 2.15 us -> 0.46 us  [shards(): pl.pallas_call(gram_kernel, out_shape=(jax.ShapeDtypeStruct((160, 128), B...]
    add x1, other arithmetic: 0.96 us -> 0.05 us  [shards(): keep + lax.ppermute(give, 'dp', moves(lambda y, x, c: (y, x, 1 - c)))]
    ppermute x4, waiting for transfers between devices: 11.1 us -> 11.9 us  [shards(): total = total + lax.ppermute(total, 'dp', moves(step))]
    pallas_call x1, Pallas kernels: 1.89 us -> 1.11 us  [shards(): pl.pallas_call(features_kernel, out_shape=jax.ShapeDtypeStruct((32, 4096)...]
where the time goes in v3:
time: 69.5 us; the launch traced here: 69.3 us
  blocking collectives  20.7 us (30%)
  Pallas kernels  18.5 us (27%)
  starting transfers between devices  15.2 us (22%)
  waiting for transfers between devices  14 us (20%)
    all_to_all x1, blocking collectives, shards(): recv = lax.all_to_all(send, 'mp', 0, 0, tiled=True)  20.7 us
    ppermute x4, waiting for transfers between devices, shards(): total = total + lax.ppermute(total, 'dp', moves(step))  11.9 us
    pallas_call x1, Pallas kernels, shards(): pl.pallas_call(factor_kernel, out_shape=jax.ShapeDtypeStruct((FB, FB), F3...  11.3 us
    ppermute x4, starting transfers between devices, shards(): total = total + lax.ppermute(total, 'dp', moves(step))  8.08 us
    pallas_call x1, Pallas kernels, shards(): pl.pallas_call(project_kernel, out_shape=jax.ShapeDtypeStruct((8, 160, 12...  5.58 us
    ppermute x1, starting transfers between devices, shards(): other = lax.ppermute(total, 'dp', moves(lambda y, x, c: (y, x, 1 - c)))  4.58 us
    ppermute x1, starting transfers between devices, shards(): lax.ppermute(give, 'dp', moves(lambda y, x, c: (y, x, 1 - c)))  2.58 us
  transfers between devices with their start and end apart: 6, of which 6 were waited for; matrix products, arithmetic and copies ran while one was open for 0% of the time, Pallas kernels for 2%

profile of v3, /device:TPU:1, one launch (start us, length us, event | category | flops | bytes accessed | tf_op | source)
XLA Modules:
  0.0 69.3 jit_solution(7535948480509114009)
XLA Ops:
  0.6 5.6 %project.1 = bf16[8,160,128]{2,1,0:T(8,128)(2,1)} custom-call(s32[128]{0:T(128)} %index_ref.1, s32[1,256]{1,0:T(1,128)} %assign_ref.1, bf16[256,1024]{1,0:T(8,128)(2,1)} %acts_hbm.1, bf16[256,3584]{1,0:T(8,128)(2,1)} %grads_hbm.1, bf16[64,8192]{1,0:T(8,128)(2,1)} %bitcast.4, bf16[128,64,128]{2,1,0:T(8,128)(2,1)} %bitcast.3), custom_call_target="tpu_custom_call" | custom-call | tf_op jit(solution)/shard_map/project/pallas_call | solution.py:262
  6.2 20.7 %all_to_all.5.recv_ref = bf16[8,160,128]{2,1,0:T(8,128)(2,1)S(1)} all-to-all(bf16[8,160,128]{2,1,0:T(8,128)(2,1)} %project.1), channel_id=1, replica_groups=mesh['dp'=32,'mp'=8] {'mp'}, dimensions={0} | all-to-all | bytes 655360 | tf_op jit(solution)/shard_map/all_to_all | solution.py:278
  27.0 0.5 gram.1
  27.4 2.6 %collective-permute-start = (bf16[640,128]{1,0:T(8,128)(2,1)S(1)}, bf16[640,128]{1,0:T(8,128)(2,1)S(1)}, u32[]{:S(2)}, u32[]{:S(2)}) collective-permute-start(bf16[640,128]{1,0:T(8,128)(2,1)S(1)} %get-tuple-element.14), channel_id=1, source_target_pairs={{0,8},{8,0},{16,24},{24,16},{32,40},{40,32},{48,56},{56,48},{64,72... | collective-permute-start | bytes 491528 | tf_op jit(solution)/shard_map/ppermute | solution.py:301
  30.0 1.0 %collective-permute-done = bf16[640,128]{1,0:T(8,128)(2,1)S(1)} collective-permute-done((bf16[640,128]{1,0:T(8,128)(2,1)S(1)}, bf16[640,128]{1,0:T(8,128)(2,1)S(1)}, u32[]{:S(2)}, u32[]{:S(2)}) %collective-permute-start) | collective-permute-done | bytes 163872 | tf_op jit(solution)/shard_map/ppermute | solution.py:301
  31.1 1.3 %collective-permute-start.1 = (bf16[640,128]{1,0:T(8,128)(2,1)S(1)}, bf16[640,128]{1,0:T(8,128)(2,1)S(1)}, u32[]{:S(2)}, u32[]{:S(2)}) collective-permute-start(bf16[640,128]{1,0:T(8,128)(2,1)S(1)} %add.15), channel_id=1, source_target_pairs={{0,16},{8,24},{16,0},{24,8},{32,48},{40,56},{48,32},{56,40},{64,80... | collective-permute-start | bytes 491528 | tf_op jit(solution)/shard_map/ppermute | solution.py:308
  32.4 1.1 %features.1 = bf16[32,4096]{1,0:T(8,128)(2,1)} custom-call(bf16[160,128]{1,0:T(8,128)(2,1)S(1)} %get-tuple-element.15.coords_ref), custom_call_target="tpu_custom_call" | custom-call | flops 16777216 | bytes 300000 | tf_op jit(solution)/shard_map/features/pallas_call | solution.py:292
  33.5 3.1 %collective-permute-done.1 = bf16[640,128]{1,0:T(8,128)(2,1)S(1)} collective-permute-done((bf16[640,128]{1,0:T(8,128)(2,1)S(1)}, bf16[640,128]{1,0:T(8,128)(2,1)S(1)}, u32[]{:S(2)}, u32[]{:S(2)}) %collective-permute-start.1) | collective-permute-done | bytes 163872 | tf_op jit(solution)/shard_map/ppermute | solution.py:308
  36.6 2.6 %collective-permute-start.2 = (bf16[640,128]{1,0:T(8,128)(2,1)S(1)}, bf16[640,128]{1,0:T(8,128)(2,1)S(1)}, u32[]{:S(2)}, u32[]{:S(2)}) collective-permute-start(bf16[640,128]{1,0:T(8,128)(2,1)S(1)} %add.16), channel_id=1, source_target_pairs={{0,48},{8,56},{16,32},{24,40},{32,16},{40,24},{48,0},{56,8},{64,11... | collective-permute-start | bytes 491528 | tf_op jit(solution)/shard_map/ppermute | solution.py:308
  39.2 3.3 %collective-permute-done.2 = bf16[640,128]{1,0:T(8,128)(2,1)S(1)} collective-permute-done((bf16[640,128]{1,0:T(8,128)(2,1)S(1)}, bf16[640,128]{1,0:T(8,128)(2,1)S(1)}, u32[]{:S(2)}, u32[]{:S(2)}) %collective-permute-start.2) | collective-permute-done | bytes 163872 | tf_op jit(solution)/shard_map/ppermute | solution.py:308
  42.5 1.4 %collective-permute-start.3 = (bf16[640,128]{1,0:T(8,128)(2,1)S(1)}, bf16[640,128]{1,0:T(8,128)(2,1)S(1)}, u32[]{:S(2)}, u32[]{:S(2)}) collective-permute-start(bf16[640,128]{1,0:T(8,128)(2,1)S(1)} %add.17), channel_id=1, source_target_pairs={{0,64},{8,72},{16,80},{24,88},{32,96},{40,104},{48,112},{56,120},{... | collective-permute-start | bytes 491528 | tf_op jit(solution)/shard_map/ppermute | solution.py:308
  43.9 2.9 %collective-permute-done.3 = bf16[640,128]{1,0:T(8,128)(2,1)S(1)} collective-permute-done((bf16[640,128]{1,0:T(8,128)(2,1)S(1)}, bf16[640,128]{1,0:T(8,128)(2,1)S(1)}, u32[]{:S(2)}, u32[]{:S(2)}) %collective-permute-start.3) | collective-permute-done | bytes 163872 | tf_op jit(solution)/shard_map/ppermute | solution.py:308
  46.8 2.8 %collective-permute-start.4 = (bf16[640,128]{1,0:T(8,128)(2,1)S(1)}, bf16[640,128]{1,0:T(8,128)(2,1)S(1)}, u32[]{:S(2)}, u32[]{:S(2)}) collective-permute-start(bf16[640,128]{1,0:T(8,128)(2,1)S(1)} %add.18), channel_id=1, source_target_pairs={{0,192},{8,200},{16,208},{24,216},{32,224},{40,232},{48,240},{56,2... | collective-permute-start | bytes 491528 | tf_op jit(solution)/shard_map/ppermute | solution.py:308
  49.6 2.7 %collective-permute-done.4 = bf16[640,128]{1,0:T(8,128)(2,1)S(1)} collective-permute-done((bf16[640,128]{1,0:T(8,128)(2,1)S(1)}, bf16[640,128]{1,0:T(8,128)(2,1)S(1)}, u32[]{:S(2)}, u32[]{:S(2)}) %collective-permute-start.4) | collective-permute-done | bytes 163872 | tf_op jit(solution)/shard_map/ppermute | solution.py:308
  52.4 4.6 %collective-permute-start.5 = (bf16[640,128]{1,0:T(8,128)(2,1)S(1)}, bf16[640,128]{1,0:T(8,128)(2,1)S(1)}, u32[]{:S(2)}, u32[]{:S(2)}) collective-permute-start(bf16[640,128]{1,0:T(8,128)(2,1)S(1)} %add.19.total_ref), channel_id=1, source_target_pairs={{0,8},{8,0},{16,24},{24,16},{32,40},{40,32},{48,56},{56,48},{64,72... | collective-permute-start | bytes 491528 | tf_op jit(solution)/shard_map/ppermute | solution.py:310
  57.0 1.0 %collective-permute-done.5.other_ref = bf16[640,128]{1,0:T(8,128)(2,1)S(1)} collective-permute-done((bf16[640,128]{1,0:T(8,128)(2,1)S(1)}, bf16[640,128]{1,0:T(8,128)(2,1)S(1)}, u32[]{:S(2)}, u32[]{:S(2)}) %collective-permute-start.5) | collective-permute-done | bytes 163872 | tf_op jit(solution)/shard_map/ppermute | solution.py:310
  58.0 11.3 %factor.1 = f32[512,512]{1,0:T(8,128)} custom-call(bf16[640,128]{1,0:T(8,128)(2,1)S(1)} %add.19.total_ref, bf16[640,128]{1,0:T(8,128)(2,1)S(1)} %collective-permute-done.5.other_ref), custom_call_target="tpu_custom_call" | custom-call | tf_op jit(solution)/shard_map/factor/pallas_call | solution.py:311
  (5 shorter events, 0.2 us)
Async XLA Ops:
  27.4 3.6 %collective-permute-start = (bf16[640,128]{1,0:T(8,128)(2,1)S(1)}, bf16[640,128]{1,0:T(8,128)(2,1)S(1)}, u32[]{:S(2)}, u32[]{:S(2)}) collective-permute-start(bf16[640,128]{1,0:T(8,128)(2,1)S(1)} %get-tuple-element.14), channel_id=1, source_target_pairs={{0,8},{8,0},{16,24},{24,16},{32,40},{40,32},{48,56},{56,48},{64,72... | collective-permute-start | bytes 491528 | tf_op jit(solution)/shard_map/ppermute | solution.py:301
  31.1 5.5 %collective-permute-start.1 = (bf16[640,128]{1,0:T(8,128)(2,1)S(1)}, bf16[640,128]{1,0:T(8,128)(2,1)S(1)}, u32[]{:S(2)}, u32[]{:S(2)}) collective-permute-start(bf16[640,128]{1,0:T(8,128)(2,1)S(1)} %add.15), channel_id=1, source_target_pairs={{0,16},{8,24},{16,0},{24,8},{32,48},{40,56},{48,32},{56,40},{64,80... | collective-permute-start | bytes 491528 | tf_op jit(solution)/shard_map/ppermute | solution.py:308
  36.6 5.8 %collective-permute-start.2 = (bf16[640,128]{1,0:T(8,128)(2,1)S(1)}, bf16[640,128]{1,0:T(8,128)(2,1)S(1)}, u32[]{:S(2)}, u32[]{:S(2)}) collective-permute-start(bf16[640,128]{1,0:T(8,128)(2,1)S(1)} %add.16), channel_id=1, source_target_pairs={{0,48},{8,56},{16,32},{24,40},{32,16},{40,24},{48,0},{56,8},{64,11... | collective-permute-start | bytes 491528 | tf_op jit(solution)/shard_map/ppermute | solution.py:308
  42.5 4.3 %collective-permute-start.3 = (bf16[640,128]{1,0:T(8,128)(2,1)S(1)}, bf16[640,128]{1,0:T(8,128)(2,1)S(1)}, u32[]{:S(2)}, u32[]{:S(2)}) collective-permute-start(bf16[640,128]{1,0:T(8,128)(2,1)S(1)} %add.17), channel_id=1, source_target_pairs={{0,64},{8,72},{16,80},{24,88},{32,96},{40,104},{48,112},{56,120},{... | collective-permute-start | bytes 491528 | tf_op jit(solution)/shard_map/ppermute | solution.py:308
  46.8 5.5 %collective-permute-start.4 = (bf16[640,128]{1,0:T(8,128)(2,1)S(1)}, bf16[640,128]{1,0:T(8,128)(2,1)S(1)}, u32[]{:S(2)}, u32[]{:S(2)}) collective-permute-start(bf16[640,128]{1,0:T(8,128)(2,1)S(1)} %add.18), channel_id=1, source_target_pairs={{0,192},{8,200},{16,208},{24,216},{32,224},{40,232},{48,240},{56,2... | collective-permute-start | bytes 491528 | tf_op jit(solution)/shard_map/ppermute | solution.py:308
  52.4 5.6 %collective-permute-start.5 = (bf16[640,128]{1,0:T(8,128)(2,1)S(1)}, bf16[640,128]{1,0:T(8,128)(2,1)S(1)}, u32[]{:S(2)}, u32[]{:S(2)}) collective-permute-start(bf16[640,128]{1,0:T(8,128)(2,1)S(1)} %add.19.total_ref), channel_id=1, source_target_pairs={{0,8},{8,0},{16,24},{24,16},{32,40},{40,32},{48,56},{56,48},{64,72... | collective-permute-start | bytes 491528 | tf_op jit(solution)/shard_map/ppermute | solution.py:310

commit v4 on v3

--- a/solution.py
+++ b/solution.py
@@ -18,31 +18,36 @@
     return lax.dot_general(a, b, NT, preferred_element_type=F32)
 
 
-def project_kernel(index_ref, assign_ref, acts_hbm, grads_hbm, proj_hbm, vals_hbm, send_ref,
-                   acts, grads, proj, vals, flags, sems, val_sems):
+def project_kernel(index_hbm, assign_hbm, acts_hbm, grads_hbm, proj_hbm, vals_hbm, send_ref,
+                   index, assign, acts, grads, proj, vals, flags, sems, val_sems):
     me = lax.axis_index("mp")
     k_in = acts.shape[1]
+    k_half = grads.shape[1] // 2
     blocks = val_sems.shape[0]
-    copies = (
-        pltpu.make_async_copy(proj_hbm.at[:, pl.ds(pl.multiple_of(me * k_in, 128), k_in)], proj, sems.at[0]),
-        pltpu.make_async_copy(acts_hbm, acts, sems.at[1]),
-        pltpu.make_async_copy(grads_hbm, grads, sems.at[2]),
+    in_copies = (
+        pltpu.make_async_copy(index_hbm, index, sems.at[0]),
+        pltpu.make_async_copy(proj_hbm.at[:, pl.ds(pl.multiple_of(me * k_in, 128), k_in)], proj, sems.at[1]),
+        pltpu.make_async_copy(acts_hbm, acts, sems.at[2]),
+        pltpu.make_async_copy(assign_hbm, assign, sems.at[3]),
     )
-    for copy in copies:
+    out_copies = [
+        pltpu.make_async_copy(grads_hbm.at[:, k_half * n:k_half * n + k_half],
+                              grads.at[:, k_half * n:k_half * n + k_half], sems.at[4 + n])
+        for n in range(2)
+    ]
+    for copy in (*in_copies, *out_copies):
         copy.start()
-
-    def clear(j, carry):
+    vals[...] = jnp.zeros(vals.shape, BF16)
+    for j in range(blocks):
         flags[j] = -1
-        return carry
-
-    lax.fori_loop(0, blocks, clear, 0)
+    in_copies[0].wait()
 
     def value_copy(j, t):
         return pltpu.make_async_copy(
             vals_hbm.at[t], vals.at[:, pl.ds(pl.multiple_of(j * 128, 128), 128)], val_sems.at[j])
 
     def find(t, carry):
-        j = index_ref[t] - me * blocks
+        j = index[t] - me * blocks
 
         @pl.when((j >= 0) & (j < blocks))
         def _():
@@ -51,22 +56,14 @@
 
         return carry
 
-    lax.fori_loop(0, index_ref.shape[0], find, 0)
-
-    def blank(j, carry):
-        @pl.when(flags[j] < 0)
-        def _():
-            vals[:, pl.ds(pl.multiple_of(j * 128, 128), 128)] = jnp.zeros((vals.shape[0], 128), BF16)
-
-        return carry
-
-    lax.fori_loop(0, blocks, blank, 0)
+    lax.fori_loop(0, index.shape[0], find, 0, unroll=16)
 
     examples = acts.shape[0]
+    in_copies[3].wait()
     rows = lax.broadcasted_iota(jnp.int32, (examples, examples), 0)
-    order = jnp.where(rows == assign_ref[...], 1.0, 0.0).astype(BF16)
-    copies[0].wait()
-    copies[1].wait()
+    order = jnp.where(rows == assign[...], 1.0, 0.0).astype(BF16)
+    in_copies[1].wait()
+    in_copies[2].wait()
     in_part = nt_dot(proj[...], acts[...]).astype(BF16)
     in_part = jnp.dot(in_part, order, preferred_element_type=F32)
 
@@ -77,10 +74,12 @@
 
         return carry
 
-    lax.fori_loop(0, blocks, settle, 0)
-    copies[2].wait()
-    out_part = nt_dot(vals[...], grads[...]).astype(BF16)
-    out_part = jnp.dot(out_part, order, preferred_element_type=F32)
+    lax.fori_loop(0, blocks, settle, 0, unroll=4)
+    out_copies[0].wait()
+    out_part = nt_dot(vals[:, 0:k_half], grads[:, 0:k_half])
+    out_copies[1].wait()
+    out_part = out_part + nt_dot(vals[:, k_half:2 * k_half], grads[:, k_half:2 * k_half])
+    out_part = jnp.dot(out_part.astype(BF16), order, preferred_element_type=F32)
     for c in range(send_ref.shape[0]):
         send_ref[c, 0:64, :] = out_part[:, 0:128].astype(BF16)
         send_ref[c, 64:128, :] = out_part[:, 128:256].astype(BF16)
@@ -92,6 +91,7 @@
 
 
 TILES = [(i, j) for i in range(4) for j in range(i, 4)]
+HALF = 336
 
 
 def gram_kernel(recv_ref, coords_ref, keep_ref, give_ref, ft, packed):
@@ -106,13 +106,31 @@
     for p in range(8):
         for h in range(2):
             ft[64 * p:64 * p + 64, 128 * h:128 * h + 128] = (in_t[h][p:p + 1] * out_t[h]).astype(BF16)
-    for at, (i, j) in enumerate(TILES):
-        packed[128 * at:128 * at + 128, :] = nt_dot(
-            ft[128 * i:128 * i + 128, :], ft[128 * j:128 * j + 128, :]).astype(BF16)
+    row32 = lax.broadcasted_iota(jnp.int32, (32, 128), 0)
+    lane64 = lax.rem(lax.broadcasted_iota(jnp.int32, (32, 128), 1), 64)
+    from_low = (lane64 < 32) & (row32 > lane64)
+    on_diagonal = lane64 == row32 + 32
+    left = lax.broadcasted_iota(jnp.int32, (32, 128), 1) < 64
+    for half in range(2):
+        spare = []
+        for at, (i, j) in enumerate(TILES[5 * half:5 * half + 5]):
+            tile = nt_dot(ft[128 * i:128 * i + 128, :], ft[128 * j:128 * j + 128, :])
+            for u in range(2):
+                top, low = tile[64 * u:64 * u + 32], tile[64 * u + 32:64 * u + 64]
+                one = jnp.where(from_low, pltpu.roll(low, 96, 1), top)
+                last = jnp.sum(jnp.where(on_diagonal, low, 0.0), axis=0, keepdims=True)
+                if i == j and u == 0:
+                    first = (one, last)
+                elif i == j:
+                    one = jnp.where(left, pltpu.roll(first[0], 64, 1), one)
+                    last = jnp.where(left[0:1], pltpu.roll(first[1], 64, 1), last)
+                packed[HALF * half + 64 * at + 32 * u:HALF * half + 64 * at + 32 * u + 32, :] = one.astype(BF16)
+                spare.append(last)
+        spare.append(jnp.zeros((6, 128), F32))
+        packed[HALF * half + 320:HALF * half + 336, :] = jnp.concatenate(spare, axis=0).astype(BF16)
     core = lax.rem(lax.axis_index("dp"), 2)
-    half = packed.shape[0] // 2
-    keep_ref[...] = packed[pl.ds(pl.multiple_of(core * half, half), half), :]
-    give_ref[...] = packed[pl.ds(pl.multiple_of((1 - core) * half, half), half), :]
+    keep_ref[...] = packed[pl.ds(pl.multiple_of(core * HALF, HALF), HALF), :]
+    give_ref[...] = packed[pl.ds(pl.multiple_of((1 - core) * HALF, HALF), HALF), :]
 
 
 def features_kernel(coords_ref, features_ref):
@@ -215,12 +233,34 @@
     return upper, inverse
 
 
-def factor_kernel(total_ref, other_ref, out_ref, work, inv):
+def factor_kernel(total_ref, other_ref, out_ref, packed, work, inv):
     core = lax.rem(lax.axis_index("dp"), 2)
-    half = total_ref.shape[0]
-    at0 = pl.multiple_of(core * half, half); at1 = pl.multiple_of((1 - core) * half, half)
-    work[pl.ds(at0, half), :] = total_ref[...].astype(F32) * (1.0 / 8192)
-    work[pl.ds(at1, half), :] = other_ref[...].astype(F32) * (1.0 / 8192)
+    packed[pl.ds(pl.multiple_of(core * HALF, HALF), HALF), :] = total_ref[...]
+    packed[pl.ds(pl.multiple_of((1 - core) * HALF, HALF), HALF), :] = other_ref[...]
+    unit = jnp.where(
+        lax.broadcasted_iota(jnp.int32, (128, 128), 0) == lax.broadcasted_iota(jnp.int32, (128, 128), 1),
+        1.0, 0.0).astype(BF16)
+    row32 = lax.broadcasted_iota(jnp.int32, (32, 128), 0)
+    lane128 = lax.broadcasted_iota(jnp.int32, (32, 128), 1)
+    lane64 = lax.rem(lane128, 64)
+    left = lane128 < 64
+    outer = lane64 < 32
+    for at in range(10):
+        half, spot_in = divmod(at, 5)
+        for u in range(2):
+            base = HALF * half + 64 * spot_in + 32 * u
+            raw = packed[base:base + 32, :]
+            turned = nt_dot(unit, jnp.concatenate([raw] * 4, axis=0))
+            wide = raw.astype(F32)
+            spare = packed[HALF * half + 320:HALF * half + 336, :].astype(F32)[2 * spot_in + u:2 * spot_in + u + 1]
+            own = jnp.where(left, turned[0:32], turned[64:96])
+            cross = jnp.where(left, turned[32:64], turned[96:128])
+            top = jnp.where(outer & (row32 > lane64), own, wide)
+            low = jnp.where(row32 > lane64 - 32, pltpu.roll(wide, 32, 1), own)
+            low = jnp.where(row32 == lane64 - 32, spare, low)
+            low = jnp.where(outer, cross, low)
+            work[128 * at + 64 * u:128 * at + 64 * u + 32, :] = top * (1.0 / 8192)
+            work[128 * at + 64 * u + 32:128 * at + 64 * u + 64, :] = low * (1.0 / 8192)
     place = {ij: 128 * n for n, ij in enumerate(TILES)}
     sub = lax.broadcasted_iota(jnp.int32, (8, 128), 0)
     lane = lax.broadcasted_iota(jnp.int32, (8, 128), 1)
@@ -256,36 +296,39 @@
 def shards(acts, grads, proj_in, block_vals, block_index, assign):
     ex, k_in = acts.shape
     k_out = grads.shape[1]
-    any_spec = pl.BlockSpec(memory_space=pl.ANY)
+    hbm = pl.BlockSpec(memory_space=pltpu.HBM)
     vmem = pl.BlockSpec(memory_space=pltpu.VMEM)
-    smem = pl.BlockSpec(memory_space=pltpu.SMEM)
     send = pl.pallas_call(
         project_kernel,
         out_shape=jax.ShapeDtypeStruct((8, 160, 128), BF16),
-        in_specs=[smem, vmem, any_spec, any_spec, any_spec, any_spec],
+        in_specs=[hbm] * 6,
         out_specs=vmem,
         scratch_shapes=[
+            pltpu.SMEM((block_index.shape[0],), jnp.int32),
+            pltpu.VMEM((1, ex), jnp.int32),
             pltpu.VMEM((ex, k_in), BF16),
             pltpu.VMEM((ex, k_out), BF16),
             pltpu.VMEM((64, k_in), BF16),
             pltpu.VMEM((64, k_out), BF16),
             pltpu.SMEM((k_out // 128,), jnp.int32),
-            pltpu.SemaphoreType.DMA((3,)),
+            pltpu.SemaphoreType.DMA((6,)),
             pltpu.SemaphoreType.DMA((k_out // 128,)),
         ],
+        compiler_params=pltpu.CompilerParams(vmem_limit_bytes=16 << 20),
         name="project",
-    )(block_index, assign, acts, grads, proj_in.T, jnp.swapaxes(block_vals, 1, 2))
+    )(*(pltpu.with_memory_space_constraint(x, pltpu.HBM) for x in (
+        block_index, assign, acts, grads, proj_in.T, jnp.swapaxes(block_vals, 1, 2))))
     recv = lax.all_to_all(send, "mp", 0, 0, tiled=True)
     coords, keep, give = pl.pallas_call(
         gram_kernel,
         out_shape=(
             jax.ShapeDtypeStruct((160, 128), BF16),
-            jax.ShapeDtypeStruct((640, 128), BF16),
-            jax.ShapeDtypeStruct((640, 128), BF16),
+            jax.ShapeDtypeStruct((HALF, 128), BF16),
+            jax.ShapeDtypeStruct((HALF, 128), BF16),
         ),
         in_specs=[vmem],
         out_specs=(vmem, vmem, vmem),
-        scratch_shapes=[pltpu.VMEM((FB, 256), BF16), pltpu.VMEM((1280, 128), BF16)],
+        scratch_shapes=[pltpu.VMEM((FB, 256), BF16), pltpu.VMEM((2 * HALF, 128), BF16)],
         compiler_params=pltpu.CompilerParams(vmem_limit_bytes=12 << 20),
         name="gram",
     )(recv)
@@ -313,7 +356,7 @@
         out_shape=jax.ShapeDtypeStruct((FB, FB), F32),
         in_specs=[vmem, vmem],
         out_specs=vmem,
-        scratch_shapes=[pltpu.VMEM((1280, 128), F32), pltpu.VMEM((128, 128), F32)],
+        scratch_shapes=[pltpu.VMEM((2 * HALF, 128), BF16), pltpu.VMEM((1280, 128), F32), pltpu.VMEM((128, 128), F32)],
         compiler_params=pltpu.CompilerParams(vmem_limit_bytes=12 << 20),
         name="factor",
     )(total, other).reshape(1, FB, FB)

time: 69.5 us -> 63.1 us (0.908)
  waiting for transfers between devices: 14 us -> 9.26 us
  Pallas kernels: 18.5 us -> 16.8 us
    ppermute x4, waiting for transfers between devices: 11.9 us -> 7.4 us  [shards(): total = total + lax.ppermute(total, 'dp', moves(step))]
    pallas_call x1, Pallas kernels: 5.58 us -> 3.42 us  [shards(): pl.pallas_call(project_kernel, out_shape=jax.ShapeDtypeStruct((8, 160, 12...]
where the time goes in v4:
time: 63.1 us; the launch traced here: 62.8 us
  blocking collectives  20.5 us (32%)
  Pallas kernels  16.8 us (27%)
  starting transfers between devices  15.5 us (25%)
  waiting for transfers between devices  9.26 us (15%)
  between operations  0.67 us (1%)
    all_to_all x1, blocking collectives, shards(): recv = lax.all_to_all(send, 'mp', 0, 0, tiled=True)  20.5 us
    pallas_call x1, Pallas kernels, shards(): pl.pallas_call(factor_kernel, out_shape=jax.ShapeDtypeStruct((FB, FB), F3...  11.7 us
    ppermute x4, starting transfers between devices, shards(): total = total + lax.ppermute(total, 'dp', moves(step))  8.07 us
    ppermute x4, waiting for transfers between devices, shards(): total = total + lax.ppermute(total, 'dp', moves(step))  7.4 us
    ppermute x1, starting transfers between devices, shards(): other = lax.ppermute(total, 'dp', moves(lambda y, x, c: (y, x, 1 - c)))  4.86 us
    pallas_call x1, Pallas kernels, shards(): pl.pallas_call(project_kernel, out_shape=jax.ShapeDtypeStruct((8, 160, 12...  3.42 us
    ppermute x1, starting transfers between devices, shards(): lax.ppermute(give, 'dp', moves(lambda y, x, c: (y, x, 1 - c)))  2.55 us
  transfers between devices with their start and end apart: 6, of which 6 were waited for; matrix products, arithmetic and copies ran while one was open for 0% of the time, Pallas kernels for 2%

profile of v4, /device:TPU:1, one launch (start us, length us, event | category | flops | bytes accessed | tf_op | source)
XLA Modules:
  0.0 62.8 jit_solution(6539579775388203734)
XLA Ops:
  0.6 3.4 %project.1 = bf16[8,160,128]{2,1,0:T(8,128)(2,1)S(1)} custom-call(s32[128]{0:T(128)} %index_hbm.1, s32[1,256]{1,0:T(1,128)} %assign_hbm.1, bf16[256,1024]{1,0:T(8,128)(2,1)} %acts_hbm.1, bf16[256,3584]{1,0:T(8,128)(2,1)} %grads_hbm.1, bf16[64,8192]{1,0:T(8,128)(2,1)} %bitcast.4, bf16[128,64,128]{2,1,0:T(8,128)(2,1)} %bitcast.3), custom_call_target="tpu_custom_call" | custom-call | tf_op jit(solution)/shard_map/project/pallas_call | solution.py:301
  4.1 20.5 %all_to_all.5.recv_ref = bf16[8,160,128]{2,1,0:T(8,128)(2,1)S(1)} all-to-all(bf16[8,160,128]{2,1,0:T(8,128)(2,1)S(1)} %project.1), channel_id=1, replica_groups=mesh['dp'=32,'mp'=8] {'mp'}, dimensions={0} | all-to-all | bytes 655360 | tf_op jit(solution)/shard_map/all_to_all | solution.py:321
  24.6 0.5 gram.1
  25.1 2.5 %collective-permute-start = (bf16[336,128]{1,0:T(8,128)(2,1)S(1)}, bf16[336,128]{1,0:T(8,128)(2,1)S(1)}, u32[]{:S(2)}, u32[]{:S(2)}) collective-permute-start(bf16[336,128]{1,0:T(8,128)(2,1)S(1)} %get-tuple-element.14), channel_id=1, source_target_pairs={{0,8},{8,0},{16,24},{24,16},{32,40},{40,32},{48,56},{56,48},{64,72... | collective-permute-start | bytes 258056 | tf_op jit(solution)/shard_map/ppermute | solution.py:344
  27.7 0.9 %collective-permute-done = bf16[336,128]{1,0:T(8,128)(2,1)S(1)} collective-permute-done((bf16[336,128]{1,0:T(8,128)(2,1)S(1)}, bf16[336,128]{1,0:T(8,128)(2,1)S(1)}, u32[]{:S(2)}, u32[]{:S(2)}) %collective-permute-start) | collective-permute-done | bytes 86048 | tf_op jit(solution)/shard_map/ppermute | solution.py:344
  28.6 1.3 %collective-permute-start.1 = (bf16[336,128]{1,0:T(8,128)(2,1)S(1)}, bf16[336,128]{1,0:T(8,128)(2,1)S(1)}, u32[]{:S(2)}, u32[]{:S(2)}) collective-permute-start(bf16[336,128]{1,0:T(8,128)(2,1)S(1)} %add.15), channel_id=1, source_target_pairs={{0,16},{8,24},{16,0},{24,8},{32,48},{40,56},{48,32},{56,40},{64,80... | collective-permute-start | bytes 258056 | tf_op jit(solution)/shard_map/ppermute | solution.py:351
  29.9 1.1 %features.1 = bf16[32,4096]{1,0:T(8,128)(2,1)} custom-call(bf16[160,128]{1,0:T(8,128)(2,1)S(1)} %get-tuple-element.15.coords_ref), custom_call_target="tpu_custom_call" | custom-call | flops 16777216 | bytes 300000 | tf_op jit(solution)/shard_map/features/pallas_call | solution.py:335
  31.0 1.4 %collective-permute-done.1 = bf16[336,128]{1,0:T(8,128)(2,1)S(1)} collective-permute-done((bf16[336,128]{1,0:T(8,128)(2,1)S(1)}, bf16[336,128]{1,0:T(8,128)(2,1)S(1)}, u32[]{:S(2)}, u32[]{:S(2)}) %collective-permute-start.1) | collective-permute-done | bytes 86048 | tf_op jit(solution)/shard_map/ppermute | solution.py:351
  32.5 2.6 %collective-permute-start.2 = (bf16[336,128]{1,0:T(8,128)(2,1)S(1)}, bf16[336,128]{1,0:T(8,128)(2,1)S(1)}, u32[]{:S(2)}, u32[]{:S(2)}) collective-permute-start(bf16[336,128]{1,0:T(8,128)(2,1)S(1)} %add.16), channel_id=1, source_target_pairs={{0,48},{8,56},{16,32},{24,40},{32,16},{40,24},{48,0},{56,8},{64,11... | collective-permute-start | bytes 258056 | tf_op jit(solution)/shard_map/ppermute | solution.py:351
  35.0 2.1 %collective-permute-done.2 = bf16[336,128]{1,0:T(8,128)(2,1)S(1)} collective-permute-done((bf16[336,128]{1,0:T(8,128)(2,1)S(1)}, bf16[336,128]{1,0:T(8,128)(2,1)S(1)}, u32[]{:S(2)}, u32[]{:S(2)}) %collective-permute-start.2) | collective-permute-done | bytes 86048 | tf_op jit(solution)/shard_map/ppermute | solution.py:351
  37.1 1.4 %collective-permute-start.3 = (bf16[336,128]{1,0:T(8,128)(2,1)S(1)}, bf16[336,128]{1,0:T(8,128)(2,1)S(1)}, u32[]{:S(2)}, u32[]{:S(2)}) collective-permute-start(bf16[336,128]{1,0:T(8,128)(2,1)S(1)} %add.17), channel_id=1, source_target_pairs={{0,64},{8,72},{16,80},{24,88},{32,96},{40,104},{48,112},{56,120},{... | collective-permute-start | bytes 258056 | tf_op jit(solution)/shard_map/ppermute | solution.py:351
  38.5 2.0 %collective-permute-done.3 = bf16[336,128]{1,0:T(8,128)(2,1)S(1)} collective-permute-done((bf16[336,128]{1,0:T(8,128)(2,1)S(1)}, bf16[336,128]{1,0:T(8,128)(2,1)S(1)}, u32[]{:S(2)}, u32[]{:S(2)}) %collective-permute-start.3) | collective-permute-done | bytes 86048 | tf_op jit(solution)/shard_map/ppermute | solution.py:351
  40.6 2.8 %collective-permute-start.4 = (bf16[336,128]{1,0:T(8,128)(2,1)S(1)}, bf16[336,128]{1,0:T(8,128)(2,1)S(1)}, u32[]{:S(2)}, u32[]{:S(2)}) collective-permute-start(bf16[336,128]{1,0:T(8,128)(2,1)S(1)} %add.18), channel_id=1, source_target_pairs={{0,192},{8,200},{16,208},{24,216},{32,224},{40,232},{48,240},{56,2... | collective-permute-start | bytes 258056 | tf_op jit(solution)/shard_map/ppermute | solution.py:351
  43.4 1.9 %collective-permute-done.4 = bf16[336,128]{1,0:T(8,128)(2,1)S(1)} collective-permute-done((bf16[336,128]{1,0:T(8,128)(2,1)S(1)}, bf16[336,128]{1,0:T(8,128)(2,1)S(1)}, u32[]{:S(2)}, u32[]{:S(2)}) %collective-permute-start.4) | collective-permute-done | bytes 86048 | tf_op jit(solution)/shard_map/ppermute | solution.py:351
  45.3 4.9 %collective-permute-start.5 = (bf16[336,128]{1,0:T(8,128)(2,1)S(1)}, bf16[336,128]{1,0:T(8,128)(2,1)S(1)}, u32[]{:S(2)}, u32[]{:S(2)}) collective-permute-start(bf16[336,128]{1,0:T(8,128)(2,1)S(1)} %add.19.total_ref), channel_id=1, source_target_pairs={{0,8},{8,0},{16,24},{24,16},{32,40},{40,32},{48,56},{56,48},{64,72... | collective-permute-start | bytes 258056 | tf_op jit(solution)/shard_map/ppermute | solution.py:353
  50.2 0.9 %collective-permute-done.5.other_ref = bf16[336,128]{1,0:T(8,128)(2,1)S(1)} collective-permute-done((bf16[336,128]{1,0:T(8,128)(2,1)S(1)}, bf16[336,128]{1,0:T(8,128)(2,1)S(1)}, u32[]{:S(2)}, u32[]{:S(2)}) %collective-permute-start.5) | collective-permute-done | bytes 86048 | tf_op jit(solution)/shard_map/ppermute | solution.py:353
  51.1 11.7 %factor.1 = f32[512,512]{1,0:T(8,128)} custom-call(bf16[336,128]{1,0:T(8,128)(2,1)S(1)} %add.19.total_ref, bf16[336,128]{1,0:T(8,128)(2,1)S(1)} %collective-permute-done.5.other_ref), custom_call_target="tpu_custom_call" | custom-call | tf_op jit(solution)/shard_map/factor/pallas_call | solution.py:354
  (5 shorter events, 0.1 us)
Async XLA Ops:
  25.1 3.5 %collective-permute-start = (bf16[336,128]{1,0:T(8,128)(2,1)S(1)}, bf16[336,128]{1,0:T(8,128)(2,1)S(1)}, u32[]{:S(2)}, u32[]{:S(2)}) collective-permute-start(bf16[336,128]{1,0:T(8,128)(2,1)S(1)} %get-tuple-element.14), channel_id=1, source_target_pairs={{0,8},{8,0},{16,24},{24,16},{32,40},{40,32},{48,56},{56,48},{64,72... | collective-permute-start | bytes 258056 | tf_op jit(solution)/shard_map/ppermute | solution.py:344
  28.6 3.8 %collective-permute-start.1 = (bf16[336,128]{1,0:T(8,128)(2,1)S(1)}, bf16[336,128]{1,0:T(8,128)(2,1)S(1)}, u32[]{:S(2)}, u32[]{:S(2)}) collective-permute-start(bf16[336,128]{1,0:T(8,128)(2,1)S(1)} %add.15), channel_id=1, source_target_pairs={{0,16},{8,24},{16,0},{24,8},{32,48},{40,56},{48,32},{56,40},{64,80... | collective-permute-start | bytes 258056 | tf_op jit(solution)/shard_map/ppermute | solution.py:351
  32.5 4.6 %collective-permute-start.2 = (bf16[336,128]{1,0:T(8,128)(2,1)S(1)}, bf16[336,128]{1,0:T(8,128)(2,1)S(1)}, u32[]{:S(2)}, u32[]{:S(2)}) collective-permute-start(bf16[336,128]{1,0:T(8,128)(2,1)S(1)} %add.16), channel_id=1, source_target_pairs={{0,48},{8,56},{16,32},{24,40},{32,16},{40,24},{48,0},{56,8},{64,11... | collective-permute-start | bytes 258056 | tf_op jit(solution)/shard_map/ppermute | solution.py:351
  37.1 3.4 %collective-permute-start.3 = (bf16[336,128]{1,0:T(8,128)(2,1)S(1)}, bf16[336,128]{1,0:T(8,128)(2,1)S(1)}, u32[]{:S(2)}, u32[]{:S(2)}) collective-permute-start(bf16[336,128]{1,0:T(8,128)(2,1)S(1)} %add.17), channel_id=1, source_target_pairs={{0,64},{8,72},{16,80},{24,88},{32,96},{40,104},{48,112},{56,120},{... | collective-permute-start | bytes 258056 | tf_op jit(solution)/shard_map/ppermute | solution.py:351
  40.6 4.7 %collective-permute-start.4 = (bf16[336,128]{1,0:T(8,128)(2,1)S(1)}, bf16[336,128]{1,0:T(8,128)(2,1)S(1)}, u32[]{:S(2)}, u32[]{:S(2)}) collective-permute-start(bf16[336,128]{1,0:T(8,128)(2,1)S(1)} %add.18), channel_id=1, source_target_pairs={{0,192},{8,200},{16,208},{24,216},{32,224},{40,232},{48,240},{56,2... | collective-permute-start | bytes 258056 | tf_op jit(solution)/shard_map/ppermute | solution.py:351
  45.3 5.8 %collective-permute-start.5 = (bf16[336,128]{1,0:T(8,128)(2,1)S(1)}, bf16[336,128]{1,0:T(8,128)(2,1)S(1)}, u32[]{:S(2)}, u32[]{:S(2)}) collective-permute-start(bf16[336,128]{1,0:T(8,128)(2,1)S(1)} %add.19.total_ref), channel_id=1, source_target_pairs={{0,8},{8,0},{16,24},{24,16},{32,40},{40,32},{48,56},{56,48},{64,72... | collective-permute-start | bytes 258056 | tf_op jit(solution)/shard_map/ppermute | solution.py:353

commit v5 on v4

--- a/solution.py
+++ b/solution.py
@@ -342,13 +342,10 @@
         name="features",
     )(coords)
     total = keep + lax.ppermute(give, "dp", moves(lambda y, x, c: (y, x, 1 - c)))
-    for step in (
-        lambda y, x, c: (y, x ^ 1, c),
-        lambda y, x, c: (y, 3 - x, c),
-        lambda y, x, c: (y ^ 1, x, c),
-        lambda y, x, c: (3 - y, x, c),
-    ):
-        total = total + lax.ppermute(total, "dp", moves(step))
+    for ring in (lambda y, x, c, k: (y, (x + k) % 4, c), lambda y, x, c, k: ((y + k) % 4, x, c)):
+        after, before, across = (
+            lax.ppermute(total, "dp", moves(functools.partial(ring, k=k))).astype(F32) for k in (1, 3, 2))
+        total = ((total.astype(F32) + across) + (after + before)).astype(BF16)
         total, features = lax.optimization_barrier((total, features))
     other = lax.ppermute(total, "dp", moves(lambda y, x, c: (y, x, 1 - c)))
     factor = pl.pallas_call(

time: 63.1 us -> 62.2 us (0.986)
    ppermute x1, starting transfers between devices: 4.86 us -> 3.64 us  [shards(): other = lax.ppermute(total, 'dp', moves(lambda y, x, c: (y, x, 1 - c)))]
    ppermute x4 -> x6, starting transfers between devices: 8.07 us -> 8.75 us  [shards(): lax.ppermute(total, 'dp', moves(functools.partial(ring, k=k))).astype(F32)]
    ppermute x4 -> x6, waiting for transfers between devices: 7.4 us -> 7.04 us  [shards(): lax.ppermute(total, 'dp', moves(functools.partial(ring, k=k))).astype(F32)]
  transfers between devices with their start and end apart: 6 -> 8, of which waited for: 6 -> 5; matrix products, arithmetic and copies ran while one was open for 0% -> 0% of each run, Pallas kernels for 2% -> 2%
where the time goes in v5:
time: 62.2 us; the launch traced here: 62 us
  blocking collectives  20.5 us (33%)
  Pallas kernels  16.8 us (27%)
  starting transfers between devices  15 us (24%)
  waiting for transfers between devices  8.9 us (14%)
  between operations  0.66 us (1%)
    all_to_all x1, blocking collectives, shards(): recv = lax.all_to_all(send, 'mp', 0, 0, tiled=True)  20.5 us
    pallas_call x1, Pallas kernels, shards(): pl.pallas_call(factor_kernel, out_shape=jax.ShapeDtypeStruct((FB, FB), F3...  11.7 us
    ppermute x6, starting transfers between devices, shards(): lax.ppermute(total, 'dp', moves(functools.partial(ring, k=k))).astype(F32)  8.75 us
    ppermute x6, waiting for transfers between devices, shards(): lax.ppermute(total, 'dp', moves(functools.partial(ring, k=k))).astype(F32)  7.04 us
    ppermute x1, starting transfers between devices, shards(): other = lax.ppermute(total, 'dp', moves(lambda y, x, c: (y, x, 1 - c)))  3.64 us
    pallas_call x1, Pallas kernels, shards(): pl.pallas_call(project_kernel, out_shape=jax.ShapeDtypeStruct((8, 160, 12...  3.39 us
    ppermute x1, starting transfers between devices, shards(): lax.ppermute(give, 'dp', moves(lambda y, x, c: (y, x, 1 - c)))  2.58 us
  transfers between devices with their start and end apart: 8, of which 5 were waited for; matrix products, arithmetic and copies ran while one was open for 0% of the time, Pallas kernels for 2%

profile of v5, /device:TPU:1, one launch (start us, length us, event | category | flops | bytes accessed | tf_op | source)
XLA Modules:
  0.0 62.0 jit_solution(15246931673806603740)
XLA Ops:
  0.6 3.4 %project.1 = bf16[8,160,128]{2,1,0:T(8,128)(2,1)S(1)} custom-call(s32[128]{0:T(128)} %index_hbm.1, s32[1,256]{1,0:T(1,128)} %assign_hbm.1, bf16[256,1024]{1,0:T(8,128)(2,1)} %acts_hbm.1, bf16[256,3584]{1,0:T(8,128)(2,1)} %grads_hbm.1, bf16[64,8192]{1,0:T(8,128)(2,1)} %bitcast.4, bf16[128,64,128]{2,1,0:T(8,128)(2,1)} %bitcast.3), custom_call_target="tpu_custom_call" | custom-call | tf_op jit(solution)/shard_map/project/pallas_call | solution.py:301
  4.0 20.5 %all_to_all.5.recv_ref = bf16[8,160,128]{2,1,0:T(8,128)(2,1)S(1)} all-to-all(bf16[8,160,128]{2,1,0:T(8,128)(2,1)S(1)} %project.1), channel_id=1, replica_groups=mesh['dp'=32,'mp'=8] {'mp'}, dimensions={0} | all-to-all | bytes 655360 | tf_op jit(solution)/shard_map/all_to_all | solution.py:321
  24.6 0.5 gram.1
  25.1 2.6 %collective-permute-start = (bf16[336,128]{1,0:T(8,128)(2,1)S(1)}, bf16[336,128]{1,0:T(8,128)(2,1)S(1)}, u32[]{:S(2)}, u32[]{:S(2)}) collective-permute-start(bf16[336,128]{1,0:T(8,128)(2,1)S(1)} %get-tuple-element.10), channel_id=1, source_target_pairs={{0,8},{8,0},{16,24},{24,16},{32,40},{40,32},{48,56},{56,48},{64,72... | collective-permute-start | bytes 258056 | tf_op jit(solution)/shard_map/ppermute | solution.py:344
  27.7 0.9 %collective-permute-done = bf16[336,128]{1,0:T(8,128)(2,1)S(1)} collective-permute-done((bf16[336,128]{1,0:T(8,128)(2,1)S(1)}, bf16[336,128]{1,0:T(8,128)(2,1)S(1)}, u32[]{:S(2)}, u32[]{:S(2)}) %collective-permute-start) | collective-permute-done | bytes 86048 | tf_op jit(solution)/shard_map/ppermute | solution.py:344
  28.6 2.6 %collective-permute-start.3 = (bf16[336,128]{1,0:T(8,128)(2,1)S(1)}, bf16[336,128]{1,0:T(8,128)(2,1)S(1)}, u32[]{:S(2)}, u32[]{:S(2)}) collective-permute-start(bf16[336,128]{1,0:T(8,128)(2,1)S(1)} %add.21), channel_id=1, source_target_pairs={{0,48},{8,56},{16,0},{24,8},{32,16},{40,24},{48,32},{56,40},{64,11... | collective-permute-start | bytes 258056 | tf_op jit(solution)/shard_map/ppermute | solution.py:347
  31.2 0.0 collective-permute-start.2
  31.2 1.7 %collective-permute-start.1 = (bf16[336,128]{1,0:T(8,128)(2,1)S(1)}, bf16[336,128]{1,0:T(8,128)(2,1)S(1)}, u32[]{:S(2)}, u32[]{:S(2)}) collective-permute-start(bf16[336,128]{1,0:T(8,128)(2,1)S(1)} %add.21), channel_id=1, source_target_pairs={{0,32},{8,40},{16,48},{24,56},{32,0},{40,8},{48,16},{56,24},{64,96... | collective-permute-start | bytes 258056 | tf_op jit(solution)/shard_map/ppermute | solution.py:347
  32.9 1.1 %features.1 = bf16[32,4096]{1,0:T(8,128)(2,1)} custom-call(bf16[160,128]{1,0:T(8,128)(2,1)S(1)} %get-tuple-element.11.coords_ref), custom_call_target="tpu_custom_call" | custom-call | flops 16777216 | bytes 300000 | tf_op jit(solution)/shard_map/features/pallas_call | solution.py:335
  34.0 0.0 collective-permute-done.3
  34.0 3.0 %collective-permute-done.2 = bf16[336,128]{1,0:T(8,128)(2,1)S(1)} collective-permute-done((bf16[336,128]{1,0:T(8,128)(2,1)S(1)}, bf16[336,128]{1,0:T(8,128)(2,1)S(1)}, u32[]{:S(2)}, u32[]{:S(2)}) %collective-permute-start.2) | collective-permute-done | bytes 86048 | tf_op jit(solution)/shard_map/ppermute | solution.py:347
  37.0 0.2 collective-permute-done.1
  37.3 2.8 %collective-permute-start.6 = (bf16[336,128]{1,0:T(8,128)(2,1)S(1)}, bf16[336,128]{1,0:T(8,128)(2,1)S(1)}, u32[]{:S(2)}, u32[]{:S(2)}) collective-permute-start(bf16[336,128]{1,0:T(8,128)(2,1)S(1)} %add_convert_fusion.1), channel_id=1, source_target_pairs={{0,192},{8,200},{16,208},{24,216},{32,224},{40,232},{48,240},{56,2... | collective-permute-start | bytes 258056 | tf_op jit(solution)/shard_map/ppermute | solution.py:347
  40.1 0.0 collective-permute-start.5
  40.1 1.6 %collective-permute-start.4 = (bf16[336,128]{1,0:T(8,128)(2,1)S(1)}, bf16[336,128]{1,0:T(8,128)(2,1)S(1)}, u32[]{:S(2)}, u32[]{:S(2)}) collective-permute-start(bf16[336,128]{1,0:T(8,128)(2,1)S(1)} %add_convert_fusion.1), channel_id=1, source_target_pairs={{0,128},{8,136},{16,144},{24,152},{32,160},{40,168},{48,176},{56,1... | collective-permute-start | bytes 258056 | tf_op jit(solution)/shard_map/ppermute | solution.py:347
  41.8 0.0 collective-permute-done.6
  41.8 3.8 %collective-permute-done.5 = bf16[336,128]{1,0:T(8,128)(2,1)S(1)} collective-permute-done((bf16[336,128]{1,0:T(8,128)(2,1)S(1)}, bf16[336,128]{1,0:T(8,128)(2,1)S(1)}, u32[]{:S(2)}, u32[]{:S(2)}) %collective-permute-start.5) | collective-permute-done | bytes 86048 | tf_op jit(solution)/shard_map/ppermute | solution.py:347
  45.6 0.0 collective-permute-done.4
  45.6 3.6 %collective-permute-start.7 = (bf16[336,128]{1,0:T(8,128)(2,1)S(1)}, bf16[336,128]{1,0:T(8,128)(2,1)S(1)}, u32[]{:S(2)}, u32[]{:S(2)}) collective-permute-start(bf16[336,128]{1,0:T(8,128)(2,1)S(1)} %add_convert_fusion.total_ref), channel_id=1, source_target_pairs={{0,8},{8,0},{16,24},{24,16},{32,40},{40,32},{48,56},{56,48},{64,72... | collective-permute-start | bytes 258056 | tf_op jit(solution)/shard_map/ppermute | solution.py:350
  49.3 0.9 %collective-permute-done.7.other_ref = bf16[336,128]{1,0:T(8,128)(2,1)S(1)} collective-permute-done((bf16[336,128]{1,0:T(8,128)(2,1)S(1)}, bf16[336,128]{1,0:T(8,128)(2,1)S(1)}, u32[]{:S(2)}, u32[]{:S(2)}) %collective-permute-start.7) | collective-permute-done | bytes 86048 | tf_op jit(solution)/shard_map/ppermute | solution.py:350
  50.2 11.7 %factor.1 = f32[512,512]{1,0:T(8,128)} custom-call(bf16[336,128]{1,0:T(8,128)(2,1)S(1)} %add_convert_fusion.total_ref, bf16[336,128]{1,0:T(8,128)(2,1)S(1)} %collective-permute-done.7.other_ref), custom_call_target="tpu_custom_call" | custom-call | tf_op jit(solution)/shard_map/factor/pallas_call | solution.py:351
  (3 shorter events, 0.1 us)
Async XLA Ops:
  25.1 3.5 %collective-permute-start = (bf16[336,128]{1,0:T(8,128)(2,1)S(1)}, bf16[336,128]{1,0:T(8,128)(2,1)S(1)}, u32[]{:S(2)}, u32[]{:S(2)}) collective-permute-start(bf16[336,128]{1,0:T(8,128)(2,1)S(1)} %get-tuple-element.10), channel_id=1, source_target_pairs={{0,8},{8,0},{16,24},{24,16},{32,40},{40,32},{48,56},{56,48},{64,72... | collective-permute-start | bytes 258056 | tf_op jit(solution)/shard_map/ppermute | solution.py:344
  28.6 5.4 %collective-permute-start.3 = (bf16[336,128]{1,0:T(8,128)(2,1)S(1)}, bf16[336,128]{1,0:T(8,128)(2,1)S(1)}, u32[]{:S(2)}, u32[]{:S(2)}) collective-permute-start(bf16[336,128]{1,0:T(8,128)(2,1)S(1)} %add.21), channel_id=1, source_target_pairs={{0,48},{8,56},{16,0},{24,8},{32,16},{40,24},{48,32},{56,40},{64,11... | collective-permute-start | bytes 258056 | tf_op jit(solution)/shard_map/ppermute | solution.py:347
  31.2 5.9 %collective-permute-start.2 = (bf16[336,128]{1,0:T(8,128)(2,1)S(1)}, bf16[336,128]{1,0:T(8,128)(2,1)S(1)}, u32[]{:S(2)}, u32[]{:S(2)}) collective-permute-start(bf16[336,128]{1,0:T(8,128)(2,1)S(1)} %add.21), channel_id=1, source_target_pairs={{0,16},{8,24},{16,32},{24,40},{32,48},{40,56},{48,0},{56,8},{64,80... | collective-permute-start | bytes 258056 | tf_op jit(solution)/shard_map/ppermute | solution.py:347
  31.2 6.1 %collective-permute-start.1 = (bf16[336,128]{1,0:T(8,128)(2,1)S(1)}, bf16[336,128]{1,0:T(8,128)(2,1)S(1)}, u32[]{:S(2)}, u32[]{:S(2)}) collective-permute-start(bf16[336,128]{1,0:T(8,128)(2,1)S(1)} %add.21), channel_id=1, source_target_pairs={{0,32},{8,40},{16,48},{24,56},{32,0},{40,8},{48,16},{56,24},{64,96... | collective-permute-start | bytes 258056 | tf_op jit(solution)/shard_map/ppermute | solution.py:347
  37.3 4.5 %collective-permute-start.6 = (bf16[336,128]{1,0:T(8,128)(2,1)S(1)}, bf16[336,128]{1,0:T(8,128)(2,1)S(1)}, u32[]{:S(2)}, u32[]{:S(2)}) collective-permute-start(bf16[336,128]{1,0:T(8,128)(2,1)S(1)} %add_convert_fusion.1), channel_id=1, source_target_pairs={{0,192},{8,200},{16,208},{24,216},{32,224},{40,232},{48,240},{56,2... | collective-permute-start | bytes 258056 | tf_op jit(solution)/shard_map/ppermute | solution.py:347
  40.1 5.5 %collective-permute-start.5 = (bf16[336,128]{1,0:T(8,128)(2,1)S(1)}, bf16[336,128]{1,0:T(8,128)(2,1)S(1)}, u32[]{:S(2)}, u32[]{:S(2)}) collective-permute-start(bf16[336,128]{1,0:T(8,128)(2,1)S(1)} %add_convert_fusion.1), channel_id=1, source_target_pairs={{0,64},{8,72},{16,80},{24,88},{32,96},{40,104},{48,112},{56,120},{... | collective-permute-start | bytes 258056 | tf_op jit(solution)/shard_map/ppermute | solution.py:347
  40.1 5.5 %collective-permute-start.4 = (bf16[336,128]{1,0:T(8,128)(2,1)S(1)}, bf16[336,128]{1,0:T(8,128)(2,1)S(1)}, u32[]{:S(2)}, u32[]{:S(2)}) collective-permute-start(bf16[336,128]{1,0:T(8,128)(2,1)S(1)} %add_convert_fusion.1), channel_id=1, source_target_pairs={{0,128},{8,136},{16,144},{24,152},{32,160},{40,168},{48,176},{56,1... | collective-permute-start | bytes 258056 | tf_op jit(solution)/shard_map/ppermute | solution.py:347
  45.6 4.6 %collective-permute-start.7 = (bf16[336,128]{1,0:T(8,128)(2,1)S(1)}, bf16[336,128]{1,0:T(8,128)(2,1)S(1)}, u32[]{:S(2)}, u32[]{:S(2)}) collective-permute-start(bf16[336,128]{1,0:T(8,128)(2,1)S(1)} %add_convert_fusion.total_ref), channel_id=1, source_target_pairs={{0,8},{8,0},{16,24},{24,16},{32,40},{40,32},{48,56},{56,48},{64,72... | collective-permute-start | bytes 258056 | tf_op jit(solution)/shard_map/ppermute | solution.py:350

commit v6 on v5

--- a/solution.py
+++ b/solution.py
@@ -19,7 +19,7 @@
 
 
 def project_kernel(index_hbm, assign_hbm, acts_hbm, grads_hbm, proj_hbm, vals_hbm, send_ref,
-                   index, assign, acts, grads, proj, vals, flags, sems, val_sems):
+                   index, assign, acts, grads, proj, vals, holder, sems, val_sems):
     me = lax.axis_index("mp")
     k_in = acts.shape[1]
     k_half = grads.shape[1] // 2
@@ -38,25 +38,25 @@
     for copy in (*in_copies, *out_copies):
         copy.start()
     vals[...] = jnp.zeros(vals.shape, BF16)
+    first = me * blocks
     for j in range(blocks):
-        flags[j] = -1
+        holder[first + j] = -1
     in_copies[0].wait()
 
-    def value_copy(j, t):
+    def record(t, carry):
+        holder[index[t]] = t
+        return carry
+
+    lax.fori_loop(0, index.shape[0], record, 0, unroll=32)
+
+    def value_copy(j):
         return pltpu.make_async_copy(
-            vals_hbm.at[t], vals.at[:, pl.ds(pl.multiple_of(j * 128, 128), 128)], val_sems.at[j])
-
-    def find(t, carry):
-        j = index[t] - me * blocks
-
-        @pl.when((j >= 0) & (j < blocks))
-        def _():
-            flags[j] = t
-            value_copy(j, t).start()
-
-        return carry
-
-    lax.fori_loop(0, index.shape[0], find, 0, unroll=16)
+            vals_hbm.at[holder[first + j]], vals.at[:, 128 * j:128 * j + 128], val_sems.at[j])
+
+    for j in range(blocks):
+        @pl.when(holder[first + j] >= 0)
+        def _(j=j):
+            value_copy(j).start()
 
     examples = acts.shape[0]
     in_copies[3].wait()
@@ -65,28 +65,26 @@
     in_copies[1].wait()
     in_copies[2].wait()
     in_part = nt_dot(proj[...], acts[...]).astype(BF16)
-    in_part = jnp.dot(in_part, order, preferred_element_type=F32)
-
-    def settle(j, carry):
-        @pl.when(flags[j] >= 0)
-        def _():
-            value_copy(j, flags[j]).wait()
-
-        return carry
-
-    lax.fori_loop(0, blocks, settle, 0, unroll=4)
+    in_order = jnp.dot(in_part, order, preferred_element_type=F32)
+    in_part = in_part.astype(F32)
+
+    for j in range(blocks):
+        @pl.when(holder[first + j] >= 0)
+        def _(j=j):
+            value_copy(j).wait()
+
     out_copies[0].wait()
     out_part = nt_dot(vals[:, 0:k_half], grads[:, 0:k_half])
     out_copies[1].wait()
     out_part = out_part + nt_dot(vals[:, k_half:2 * k_half], grads[:, k_half:2 * k_half])
-    out_part = jnp.dot(out_part.astype(BF16), order, preferred_element_type=F32)
+    out_part = out_part.astype(BF16)
     for c in range(send_ref.shape[0]):
-        send_ref[c, 0:64, :] = out_part[:, 0:128].astype(BF16)
-        send_ref[c, 64:128, :] = out_part[:, 128:256].astype(BF16)
+        send_ref[c, 0:64, :] = out_part[:, 0:128]
+        send_ref[c, 64:128, :] = out_part[:, 128:256]
         tops = jnp.concatenate([in_part[8 * c:8 * c + 8, 0:128], in_part[8 * c:8 * c + 8, 128:256]], axis=0)
         send_ref[c, 128:144, :] = tops.astype(BF16)
         mine = jnp.concatenate(
-            [in_part[16 * k:16 * k + 16, 32 * c:32 * c + 32] for k in range(4)], axis=1)
+            [in_order[16 * k:16 * k + 16, 32 * c:32 * c + 32] for k in range(4)], axis=1)
         send_ref[c, 144:160, :] = mine.astype(BF16)
 
 
@@ -133,14 +131,16 @@
     give_ref[...] = packed[pl.ds(pl.multiple_of((1 - core) * HALF, HALF), HALF), :]
 
 
-def features_kernel(coords_ref, features_ref):
+def features_kernel(assign_ref, coords_ref, features_ref):
     me = lax.axis_index("mp")
     coords = coords_ref[...]
     picked = jnp.concatenate([coords[0:64], coords[64:128]], axis=1)
     rows = lax.broadcasted_iota(jnp.int32, (32, 256), 0)
     cols = lax.broadcasted_iota(jnp.int32, (32, 256), 1)
     pick = jnp.where(cols == rows + 32 * me, 1.0, 0.0).astype(BF16)
-    outs = nt_dot(pick, picked)
+    examples = lax.broadcasted_iota(jnp.int32, (256, 256), 0)
+    order = jnp.where(examples == assign_ref[...], 1.0, 0.0).astype(BF16)
+    outs = nt_dot(pick, jnp.dot(picked, order, preferred_element_type=F32).astype(BF16))
     wide = coords[144:160].astype(F32)
     mine = jnp.concatenate([wide[:, 32 * k:32 * k + 32] for k in range(4)], axis=0).astype(BF16)
     turn = jnp.where(
@@ -164,6 +164,23 @@
 
 def row(x, j):
     return jnp.broadcast_to(x[j:j + 1, :], (8, 128))
+
+def split(x):
+    high = x.astype(BF16)
+    return high, (x - high.astype(F32)).astype(BF16)
+
+
+def close_dot(a, b, dims):
+    (ah, al), (bh, bl) = split(a), split(b)
+
+    def one(x, y):
+        return lax.dot_general(x, y, (dims, ((), ())), preferred_element_type=F32)
+
+    return one(ah, bh) + (one(ah, bl) + one(al, bh))
+
+
+NN = ((1,), (0,))
+TN = ((0,), (0,))
 
 WIDE = 16
 
@@ -226,14 +243,13 @@
             pad = [jnp.zeros((8, 128), F32)] * n
             for u in range(h):
                 pad[p + u] = dones[u]
-            change = jnp.dot(jnp.concatenate([c[t] for t in far], axis=0), jnp.concatenate(pad, axis=0),
-                             preferred_element_type=F32, precision=lax.Precision.HIGHEST)
+            change = close_dot(jnp.concatenate([c[t] for t in far], axis=0), jnp.concatenate(pad, axis=0), NN)
             for at, t in enumerate(far):
                 c[t] = jnp.where(inside, 0.0, c[t]) - change[8 * at:8 * at + 8]
     return upper, inverse
 
 
-def factor_kernel(total_ref, other_ref, out_ref, packed, work, inv):
+def factor_kernel(total_ref, other_ref, out_hbm, out, packed, work, inv, sems):
     core = lax.rem(lax.axis_index("dp"), 2)
     packed[pl.ds(pl.multiple_of(core * HALF, HALF), HALF), :] = total_ref[...]
     packed[pl.ds(pl.multiple_of((1 - core) * HALF, HALF), HALF), :] = other_ref[...]
@@ -264,25 +280,30 @@
     place = {ij: 128 * n for n, ij in enumerate(TILES)}
     sub = lax.broadcasted_iota(jnp.int32, (8, 128), 0)
     lane = lax.broadcasted_iota(jnp.int32, (8, 128), 1)
+    done = [pltpu.make_async_copy(out.at[128 * s:128 * s + 128, :], out_hbm.at[128 * s:128 * s + 128, :], sems.at[s]) for s in range(4)]
     for s in range(4):
         o = place[s, s]
         c = [work[o + 8 * t:o + 8 * t + 8, :] + jnp.where(lane == sub + 8 * t, DAMPING, 0.0) for t in range(16)]
         upper, inverse = factor_block(c)
+        if s:
+            done[s - 1].start()
         for t in range(16):
-            out_ref[128 * s + 8 * t:128 * s + 8 * t + 8, 128 * s:128 * s + 128] = upper[t]
+            out[128 * s + 8 * t:128 * s + 8 * t + 8, 128 * s:128 * s + 128] = upper[t]
             inv[8 * t:8 * t + 8, :] = inverse[t]
         for j in range(s):
-            out_ref[128 * s:128 * s + 128, 128 * j:128 * j + 128] = jnp.zeros((128, 128), F32)
+            out[128 * s:128 * s + 128, 128 * j:128 * j + 128] = jnp.zeros((128, 128), F32)
         for j in range(s + 1, 4):
             a = work[place[s, j]:place[s, j] + 128, :]
-            out_ref[128 * s:128 * s + 128, 128 * j:128 * j + 128] = jnp.dot(
-                inv[...], a, preferred_element_type=F32, precision=lax.Precision.HIGHEST)
+            out[128 * s:128 * s + 128, 128 * j:128 * j + 128] = close_dot(inv[...], a, NN)
         for i in range(s + 1, 4):
             for j in range(i, 4):
-                ri = out_ref[128 * s:128 * s + 128, 128 * i:128 * i + 128]
-                rj = out_ref[128 * s:128 * s + 128, 128 * j:128 * j + 128]
-                work[place[i, j]:place[i, j] + 128, :] -= lax.dot_general(
-                    ri, rj, (((0,), (0,)), ((), ())), preferred_element_type=F32, precision=lax.Precision.HIGHEST)
+                ri = out[128 * s:128 * s + 128, 128 * i:128 * i + 128]
+                rj = out[128 * s:128 * s + 128, 128 * j:128 * j + 128]
+                work[place[i, j]:place[i, j] + 128, :] -= close_dot(ri, rj, TN)
+    done[3].start()
+    for copy in done:
+        copy.wait()
+
 
 def spot(y, x, core):
     return (y * 4 + x) * 2 + core
@@ -296,6 +317,7 @@
 def shards(acts, grads, proj_in, block_vals, block_index, assign):
     ex, k_in = acts.shape
     k_out = grads.shape[1]
+    mp_count = lax.axis_size("mp")
     hbm = pl.BlockSpec(memory_space=pltpu.HBM)
     vmem = pl.BlockSpec(memory_space=pltpu.VMEM)
     send = pl.pallas_call(
@@ -310,7 +332,7 @@
             pltpu.VMEM((ex, k_out), BF16),
             pltpu.VMEM((64, k_in), BF16),
             pltpu.VMEM((64, k_out), BF16),
-            pltpu.SMEM((k_out // 128,), jnp.int32),
+            pltpu.SMEM((mp_count * k_out // 128,), jnp.int32),
             pltpu.SemaphoreType.DMA((6,)),
             pltpu.SemaphoreType.DMA((k_out // 128,)),
         ],
@@ -335,12 +357,12 @@
     features = pl.pallas_call(
         features_kernel,
         out_shape=jax.ShapeDtypeStruct((32, 4096), BF16),
-        in_specs=[vmem],
+        in_specs=[vmem, vmem],
         out_specs=vmem,
         cost_estimate=pl.CostEstimate(flops=2 * 32 * 64 * 4096, bytes_accessed=300000, transcendentals=0),
         compiler_params=pltpu.CompilerParams(vmem_limit_bytes=12 << 20),
         name="features",
-    )(coords)
+    )(assign, coords)
     total = keep + lax.ppermute(give, "dp", moves(lambda y, x, c: (y, x, 1 - c)))
     for ring in (lambda y, x, c, k: (y, (x + k) % 4, c), lambda y, x, c, k: ((y + k) % 4, x, c)):
         after, before, across = (
@@ -352,8 +374,14 @@
         factor_kernel,
         out_shape=jax.ShapeDtypeStruct((FB, FB), F32),
         in_specs=[vmem, vmem],
-        out_specs=vmem,
-        scratch_shapes=[pltpu.VMEM((2 * HALF, 128), BF16), pltpu.VMEM((1280, 128), F32), pltpu.VMEM((128, 128), F32)],
+        out_specs=hbm,
+        scratch_shapes=[
+            pltpu.VMEM((FB, FB), F32),
+            pltpu.VMEM((2 * HALF, 128), BF16),
+            pltpu.VMEM((1280, 128), F32),
+            pltpu.VMEM((128, 128), F32),
+            pltpu.SemaphoreType.DMA((4,)),
+        ],
         compiler_params=pltpu.CompilerParams(vmem_limit_bytes=12 << 20),
         name="factor",
     )(total, other).reshape(1, FB, FB)

time: 62.2 us -> 61.2 us (0.984)
  Pallas kernels: 16.8 us -> 15.7 us
    pallas_call x1, Pallas kernels: 11.7 us -> 10.8 us  [shards(): pl.pallas_call(factor_kernel, out_shape=jax.ShapeDtypeStruct((FB, FB), F3...]
where the time goes in v6:
time: 61.2 us; the launch traced here: 61 us
  blocking collectives  20.6 us (34%)
  Pallas kernels  15.7 us (26%)
  starting transfers between devices  14.9 us (24%)
  waiting for transfers between devices  8.78 us (14%)
  between operations  0.83 us (1%)
    all_to_all x1, blocking collectives, shards(): recv = lax.all_to_all(send, 'mp', 0, 0, tiled=True)  20.6 us
    pallas_call x1, Pallas kernels, shards(): pl.pallas_call(factor_kernel, out_shape=jax.ShapeDtypeStruct((FB, FB), F3...  10.8 us
    ppermute x6, starting transfers between devices, shards(): lax.ppermute(total, 'dp', moves(functools.partial(ring, k=k))).astype(F32)  8.75 us
    ppermute x6, waiting for transfers between devices, shards(): lax.ppermute(total, 'dp', moves(functools.partial(ring, k=k))).astype(F32)  6.93 us
    ppermute x1, starting transfers between devices, shards(): other = lax.ppermute(total, 'dp', moves(lambda y, x, c: (y, x, 1 - c)))  3.65 us
    pallas_call x1, Pallas kernels, shards(): pl.pallas_call(project_kernel, out_shape=jax.ShapeDtypeStruct((8, 160, 12...  3.22 us
    ppermute x1, starting transfers between devices, shards(): lax.ppermute(give, 'dp', moves(lambda y, x, c: (y, x, 1 - c)))  2.55 us
  transfers between devices with their start and end apart: 8, of which 5 were waited for; matrix products, arithmetic and copies ran while one was open for 0% of the time, Pallas kernels for 2%

profile of v6, /device:TPU:1, one launch (start us, length us, event | category | flops | bytes accessed | tf_op | source)
XLA Modules:
  0.0 61.0 jit_solution(129209888346876173)
XLA Ops:
  0.6 0.0 copy-start
  0.6 3.2 %project.1 = bf16[8,160,128]{2,1,0:T(8,128)(2,1)S(1)} custom-call(s32[128]{0:T(128)} %index_hbm.1, s32[1,256]{1,0:T(1,128)} %assign_ref.1, bf16[256,1024]{1,0:T(8,128)(2,1)} %acts_hbm.1, bf16[256,3584]{1,0:T(8,128)(2,1)} %grads_hbm.1, bf16[64,8192]{1,0:T(8,128)(2,1)} %bitcast.4, bf16[128,64,128]{2,1,0:T(8,128)(2,1)} %bitcast.3), custom_call_target="tpu_custom_call" | custom-call | tf_op jit(solution)/shard_map/project/pallas_call | solution.py:323
  3.9 20.6 %all_to_all.5.recv_ref = bf16[8,160,128]{2,1,0:T(8,128)(2,1)S(1)} all-to-all(bf16[8,160,128]{2,1,0:T(8,128)(2,1)S(1)} %project.1), channel_id=1, replica_groups=mesh['dp'=32,'mp'=8] {'mp'}, dimensions={0} | all-to-all | bytes 655360 | tf_op jit(solution)/shard_map/all_to_all | solution.py:343
  24.4 0.5 gram.1
  25.0 2.5 %collective-permute-start = (bf16[336,128]{1,0:T(8,128)(2,1)S(1)}, bf16[336,128]{1,0:T(8,128)(2,1)S(1)}, u32[]{:S(2)}, u32[]{:S(2)}) collective-permute-start(bf16[336,128]{1,0:T(8,128)(2,1)S(1)} %get-tuple-element.10), channel_id=1, source_target_pairs={{0,8},{8,0},{16,24},{24,16},{32,40},{40,32},{48,56},{56,48},{64,72... | collective-permute-start | bytes 258056 | tf_op jit(solution)/shard_map/ppermute | solution.py:366
  27.5 0.9 %collective-permute-done = bf16[336,128]{1,0:T(8,128)(2,1)S(1)} collective-permute-done((bf16[336,128]{1,0:T(8,128)(2,1)S(1)}, bf16[336,128]{1,0:T(8,128)(2,1)S(1)}, u32[]{:S(2)}, u32[]{:S(2)}) %collective-permute-start) | collective-permute-done | bytes 86048 | tf_op jit(solution)/shard_map/ppermute | solution.py:366
  28.5 2.6 %collective-permute-start.3 = (bf16[336,128]{1,0:T(8,128)(2,1)S(1)}, bf16[336,128]{1,0:T(8,128)(2,1)S(1)}, u32[]{:S(2)}, u32[]{:S(2)}) collective-permute-start(bf16[336,128]{1,0:T(8,128)(2,1)S(1)} %add.21), channel_id=1, source_target_pairs={{0,48},{8,56},{16,0},{24,8},{32,16},{40,24},{48,32},{56,40},{64,11... | collective-permute-start | bytes 258056 | tf_op jit(solution)/shard_map/ppermute | solution.py:369
  31.0 0.0 collective-permute-start.2
  31.0 1.7 %collective-permute-start.1 = (bf16[336,128]{1,0:T(8,128)(2,1)S(1)}, bf16[336,128]{1,0:T(8,128)(2,1)S(1)}, u32[]{:S(2)}, u32[]{:S(2)}) collective-permute-start(bf16[336,128]{1,0:T(8,128)(2,1)S(1)} %add.21), channel_id=1, source_target_pairs={{0,32},{8,40},{16,48},{24,56},{32,0},{40,8},{48,16},{56,24},{64,96... | collective-permute-start | bytes 258056 | tf_op jit(solution)/shard_map/ppermute | solution.py:369
  32.8 0.0 copy-done
  32.8 1.2 %features.1 = bf16[32,4096]{1,0:T(8,128)(2,1)} custom-call(s32[1,256]{1,0:T(1,128)S(1)} %copy-done, bf16[160,128]{1,0:T(8,128)(2,1)S(1)} %get-tuple-element.11.coords_ref), custom_call_target="tpu_custom_call" | custom-call | flops 16777216 | bytes 300000 | tf_op jit(solution)/shard_map/features/pallas_call | solution.py:357
  34.0 0.0 collective-permute-done.3
  34.0 2.9 %collective-permute-done.2 = bf16[336,128]{1,0:T(8,128)(2,1)S(1)} collective-permute-done((bf16[336,128]{1,0:T(8,128)(2,1)S(1)}, bf16[336,128]{1,0:T(8,128)(2,1)S(1)}, u32[]{:S(2)}, u32[]{:S(2)}) %collective-permute-start.2) | collective-permute-done | bytes 86048 | tf_op jit(solution)/shard_map/ppermute | solution.py:369
  36.9 0.2 collective-permute-done.1
  37.1 2.8 %collective-permute-start.6 = (bf16[336,128]{1,0:T(8,128)(2,1)S(1)}, bf16[336,128]{1,0:T(8,128)(2,1)S(1)}, u32[]{:S(2)}, u32[]{:S(2)}) collective-permute-start(bf16[336,128]{1,0:T(8,128)(2,1)S(1)} %add_convert_fusion.1), channel_id=1, source_target_pairs={{0,192},{8,200},{16,208},{24,216},{32,224},{40,232},{48,240},{56,2... | collective-permute-start | bytes 258056 | tf_op jit(solution)/shard_map/ppermute | solution.py:369
  40.0 0.0 collective-permute-start.5
  40.0 1.6 %collective-permute-start.4 = (bf16[336,128]{1,0:T(8,128)(2,1)S(1)}, bf16[336,128]{1,0:T(8,128)(2,1)S(1)}, u32[]{:S(2)}, u32[]{:S(2)}) collective-permute-start(bf16[336,128]{1,0:T(8,128)(2,1)S(1)} %add_convert_fusion.1), channel_id=1, source_target_pairs={{0,128},{8,136},{16,144},{24,152},{32,160},{40,168},{48,176},{56,1... | collective-permute-start | bytes 258056 | tf_op jit(solution)/shard_map/ppermute | solution.py:369
  41.6 0.0 collective-permute-done.6
  41.6 3.8 %collective-permute-done.5 = bf16[336,128]{1,0:T(8,128)(2,1)S(1)} collective-permute-done((bf16[336,128]{1,0:T(8,128)(2,1)S(1)}, bf16[336,128]{1,0:T(8,128)(2,1)S(1)}, u32[]{:S(2)}, u32[]{:S(2)}) %collective-permute-start.5) | collective-permute-done | bytes 86048 | tf_op jit(solution)/shard_map/ppermute | solution.py:369
  45.4 0.0 collective-permute-done.4
  45.5 3.6 %collective-permute-start.7 = (bf16[336,128]{1,0:T(8,128)(2,1)S(1)}, bf16[336,128]{1,0:T(8,128)(2,1)S(1)}, u32[]{:S(2)}, u32[]{:S(2)}) collective-permute-start(bf16[336,128]{1,0:T(8,128)(2,1)S(1)} %add_convert_fusion.total_ref), channel_id=1, source_target_pairs={{0,8},{8,0},{16,24},{24,16},{32,40},{40,32},{48,56},{56,48},{64,72... | collective-permute-start | bytes 258056 | tf_op jit(solution)/shard_map/ppermute | solution.py:372
  49.1 0.9 %collective-permute-done.7.other_ref = bf16[336,128]{1,0:T(8,128)(2,1)S(1)} collective-permute-done((bf16[336,128]{1,0:T(8,128)(2,1)S(1)}, bf16[336,128]{1,0:T(8,128)(2,1)S(1)}, u32[]{:S(2)}, u32[]{:S(2)}) %collective-permute-start.7) | collective-permute-done | bytes 86048 | tf_op jit(solution)/shard_map/ppermute | solution.py:372
  50.1 10.8 %factor.1 = f32[512,512]{1,0:T(8,128)} custom-call(bf16[336,128]{1,0:T(8,128)(2,1)S(1)} %add_convert_fusion.total_ref, bf16[336,128]{1,0:T(8,128)(2,1)S(1)} %collective-permute-done.7.other_ref), custom_call_target="tpu_custom_call" | custom-call | tf_op jit(solution)/shard_map/factor/pallas_call | solution.py:373
  (3 shorter events, 0.1 us)
Async XLA Ops:
  0.6 32.1 %copy-start = (s32[1,256]{1,0:T(1,128)S(1)}, s32[1,256]{1,0:T(1,128)}, u32[]{:S(2)}) copy-start(s32[1,256]{1,0:T(1,128)} %assign_ref.1) | copy-start | bytes 3076
  25.0 3.5 %collective-permute-start = (bf16[336,128]{1,0:T(8,128)(2,1)S(1)}, bf16[336,128]{1,0:T(8,128)(2,1)S(1)}, u32[]{:S(2)}, u32[]{:S(2)}) collective-permute-start(bf16[336,128]{1,0:T(8,128)(2,1)S(1)} %get-tuple-element.10), channel_id=1, source_target_pairs={{0,8},{8,0},{16,24},{24,16},{32,40},{40,32},{48,56},{56,48},{64,72... | collective-permute-start | bytes 258056 | tf_op jit(solution)/shard_map/ppermute | solution.py:366
  28.5 5.5 %collective-permute-start.3 = (bf16[336,128]{1,0:T(8,128)(2,1)S(1)}, bf16[336,128]{1,0:T(8,128)(2,1)S(1)}, u32[]{:S(2)}, u32[]{:S(2)}) collective-permute-start(bf16[336,128]{1,0:T(8,128)(2,1)S(1)} %add.21), channel_id=1, source_target_pairs={{0,48},{8,56},{16,0},{24,8},{32,16},{40,24},{48,32},{56,40},{64,11... | collective-permute-start | bytes 258056 | tf_op jit(solution)/shard_map/ppermute | solution.py:369
  31.0 5.9 %collective-permute-start.2 = (bf16[336,128]{1,0:T(8,128)(2,1)S(1)}, bf16[336,128]{1,0:T(8,128)(2,1)S(1)}, u32[]{:S(2)}, u32[]{:S(2)}) collective-permute-start(bf16[336,128]{1,0:T(8,128)(2,1)S(1)} %add.21), channel_id=1, source_target_pairs={{0,16},{8,24},{16,32},{24,40},{32,48},{40,56},{48,0},{56,8},{64,80... | collective-permute-start | bytes 258056 | tf_op jit(solution)/shard_map/ppermute | solution.py:369
  31.0 6.1 %collective-permute-start.1 = (bf16[336,128]{1,0:T(8,128)(2,1)S(1)}, bf16[336,128]{1,0:T(8,128)(2,1)S(1)}, u32[]{:S(2)}, u32[]{:S(2)}) collective-permute-start(bf16[336,128]{1,0:T(8,128)(2,1)S(1)} %add.21), channel_id=1, source_target_pairs={{0,32},{8,40},{16,48},{24,56},{32,0},{40,8},{48,16},{56,24},{64,96... | collective-permute-start | bytes 258056 | tf_op jit(solution)/shard_map/ppermute | solution.py:369
  37.1 4.5 %collective-permute-start.6 = (bf16[336,128]{1,0:T(8,128)(2,1)S(1)}, bf16[336,128]{1,0:T(8,128)(2,1)S(1)}, u32[]{:S(2)}, u32[]{:S(2)}) collective-permute-start(bf16[336,128]{1,0:T(8,128)(2,1)S(1)} %add_convert_fusion.1), channel_id=1, source_target_pairs={{0,192},{8,200},{16,208},{24,216},{32,224},{40,232},{48,240},{56,2... | collective-permute-start | bytes 258056 | tf_op jit(solution)/shard_map/ppermute | solution.py:369
  40.0 5.5 %collective-permute-start.5 = (bf16[336,128]{1,0:T(8,128)(2,1)S(1)}, bf16[336,128]{1,0:T(8,128)(2,1)S(1)}, u32[]{:S(2)}, u32[]{:S(2)}) collective-permute-start(bf16[336,128]{1,0:T(8,128)(2,1)S(1)} %add_convert_fusion.1), channel_id=1, source_target_pairs={{0,64},{8,72},{16,80},{24,88},{32,96},{40,104},{48,112},{56,120},{... | collective-permute-start | bytes 258056 | tf_op jit(solution)/shard_map/ppermute | solution.py:369
  40.0 5.5 %collective-permute-start.4 = (bf16[336,128]{1,0:T(8,128)(2,1)S(1)}, bf16[336,128]{1,0:T(8,128)(2,1)S(1)}, u32[]{:S(2)}, u32[]{:S(2)}) collective-permute-start(bf16[336,128]{1,0:T(8,128)(2,1)S(1)} %add_convert_fusion.1), channel_id=1, source_target_pairs={{0,128},{8,136},{16,144},{24,152},{32,160},{40,168},{48,176},{56,1... | collective-permute-start | bytes 258056 | tf_op jit(solution)/shard_map/ppermute | solution.py:369
  45.5 4.6 %collective-permute-start.7 = (bf16[336,128]{1,0:T(8,128)(2,1)S(1)}, bf16[336,128]{1,0:T(8,128)(2,1)S(1)}, u32[]{:S(2)}, u32[]{:S(2)}) collective-permute-start(bf16[336,128]{1,0:T(8,128)(2,1)S(1)} %add_convert_fusion.total_ref), channel_id=1, source_target_pairs={{0,8},{8,0},{16,24},{24,16},{32,40},{40,32},{48,56},{56,48},{64,72... | collective-permute-start | bytes 258056 | tf_op jit(solution)/shard_map/ppermute | solution.py:372

commit v7 on v6

--- a/solution.py
+++ b/solution.py
@@ -89,7 +89,8 @@
 
 
 TILES = [(i, j) for i in range(4) for j in range(i, 4)]
-HALF = 336
+HALF = 304
+SLOTS = 8
 
 
 def gram_kernel(recv_ref, coords_ref, keep_ref, give_ref, ft, packed):
@@ -110,22 +111,23 @@
     on_diagonal = lane64 == row32 + 32
     left = lax.broadcasted_iota(jnp.int32, (32, 128), 1) < 64
     for half in range(2):
-        spare = []
-        for at, (i, j) in enumerate(TILES[5 * half:5 * half + 5]):
+        spare, single, slot = [], [], 0
+        for i, j in TILES[5 * half:5 * half + 5]:
             tile = nt_dot(ft[128 * i:128 * i + 128, :], ft[128 * j:128 * j + 128, :])
             for u in range(2):
                 top, low = tile[64 * u:64 * u + 32], tile[64 * u + 32:64 * u + 64]
                 one = jnp.where(from_low, pltpu.roll(low, 96, 1), top)
-                last = jnp.sum(jnp.where(on_diagonal, low, 0.0), axis=0, keepdims=True)
-                if i == j and u == 0:
-                    first = (one, last)
-                elif i == j:
-                    one = jnp.where(left, pltpu.roll(first[0], 64, 1), one)
-                    last = jnp.where(left[0:1], pltpu.roll(first[1], 64, 1), last)
-                packed[HALF * half + 64 * at + 32 * u:HALF * half + 64 * at + 32 * u + 32, :] = one.astype(BF16)
-                spare.append(last)
+                spare.append(jnp.sum(jnp.where(on_diagonal, low, 0.0), axis=0, keepdims=True))
+                if i == j and u == 1:
+                    single.append(one)
+                    spare[-1] = jnp.where(left[0:1], pltpu.roll(spare[-2], 64, 1), spare[-1])
+                else:
+                    packed[HALF * half + 32 * slot:HALF * half + 32 * slot + 32, :] = one.astype(BF16)
+                    slot += 1
+        one = jnp.where(left, pltpu.roll(single[1], 64, 1), single[0])
+        packed[HALF * half + 32 * SLOTS:HALF * half + 32 * SLOTS + 32, :] = one.astype(BF16)
         spare.append(jnp.zeros((6, 128), F32))
-        packed[HALF * half + 320:HALF * half + 336, :] = jnp.concatenate(spare, axis=0).astype(BF16)
+        packed[HALF * half + HALF - 16:HALF * half + HALF, :] = jnp.concatenate(spare, axis=0).astype(BF16)
     core = lax.rem(lax.axis_index("dp"), 2)
     keep_ref[...] = packed[pl.ds(pl.multiple_of(core * HALF, HALF), HALF), :]
     give_ref[...] = packed[pl.ds(pl.multiple_of((1 - core) * HALF, HALF), HALF), :]
@@ -261,14 +263,24 @@
     lane64 = lax.rem(lane128, 64)
     left = lane128 < 64
     outer = lane64 < 32
-    for at in range(10):
+    slots = [0, 0]
+    for at, (i, j) in enumerate(TILES):
         half, spot_in = divmod(at, 5)
         for u in range(2):
-            base = HALF * half + 64 * spot_in + 32 * u
-            raw = packed[base:base + 32, :]
+            if i == j and u == 1:
+                first = wide
+                single = packed[HALF * half + 32 * SLOTS:HALF * half + 32 * SLOTS + 32, :].astype(F32)
+                if i % 2:
+                    single = pltpu.roll(single, 64, 1)
+                wide = jnp.where(left, pltpu.roll(first, 64, 1), single)
+                raw = wide.astype(BF16)
+            else:
+                base = HALF * half + 32 * slots[half]
+                slots[half] += 1
+                raw = packed[base:base + 32, :]
+                wide = raw.astype(F32)
             turned = nt_dot(unit, jnp.concatenate([raw] * 4, axis=0))
-            wide = raw.astype(F32)
-            spare = packed[HALF * half + 320:HALF * half + 336, :].astype(F32)[2 * spot_in + u:2 * spot_in + u + 1]
+            spare = packed[HALF * half + HALF - 16:HALF * half + HALF, :].astype(F32)[2 * spot_in + u:2 * spot_in + u + 1]
             own = jnp.where(left, turned[0:32], turned[64:96])
             cross = jnp.where(left, turned[32:64], turned[96:128])
             top = jnp.where(outer & (row32 > lane64), own, wide)

time: 61.2 us -> 60.7 us (level)
  no operation moved by 1% of the time
where the time goes in v7:
time: 60.7 us; the launch traced here: 60.5 us
  blocking collectives  20.5 us (34%)
  Pallas kernels  15.8 us (26%)
  starting transfers between devices  14.8 us (24%)
  waiting for transfers between devices  8.41 us (14%)
  between operations  0.83 us (1%)
    all_to_all x1, blocking collectives, shards(): recv = lax.all_to_all(send, 'mp', 0, 0, tiled=True)  20.5 us
    pallas_call x1, Pallas kernels, shards(): pl.pallas_call(factor_kernel, out_shape=jax.ShapeDtypeStruct((FB, FB), F3...  10.8 us
    ppermute x6, starting transfers between devices, shards(): lax.ppermute(total, 'dp', moves(functools.partial(ring, k=k))).astype(F32)  8.75 us
    ppermute x6, waiting for transfers between devices, shards(): lax.ppermute(total, 'dp', moves(functools.partial(ring, k=k))).astype(F32)  6.57 us
    ppermute x1, starting transfers between devices, shards(): other = lax.ppermute(total, 'dp', moves(lambda y, x, c: (y, x, 1 - c)))  3.47 us
    pallas_call x1, Pallas kernels, shards(): pl.pallas_call(project_kernel, out_shape=jax.ShapeDtypeStruct((8, 160, 12...  3.19 us
    ppermute x1, starting transfers between devices, shards(): lax.ppermute(give, 'dp', moves(lambda y, x, c: (y, x, 1 - c)))  2.58 us
    pallas_call x1, Pallas kernels, shards(): pl.pallas_call(features_kernel, out_shape=jax.ShapeDtypeStruct((32, 4096)...  1.22 us
  transfers between devices with their start and end apart: 8, of which 5 were waited for; matrix products, arithmetic and copies ran while one was open for 0% of the time, Pallas kernels for 2%

profile of v7, /device:TPU:1, one launch (start us, length us, event | category | flops | bytes accessed | tf_op | source)
XLA Modules:
  0.0 60.5 jit_solution(16691459356305944995)
XLA Ops:
  0.6 0.0 copy-start
  0.6 3.2 %project.1 = bf16[8,160,128]{2,1,0:T(8,128)(2,1)S(1)} custom-call(s32[128]{0:T(128)} %index_hbm.1, s32[1,256]{1,0:T(1,128)} %assign_ref.1, bf16[256,1024]{1,0:T(8,128)(2,1)} %acts_hbm.1, bf16[256,3584]{1,0:T(8,128)(2,1)} %grads_hbm.1, bf16[64,8192]{1,0:T(8,128)(2,1)} %bitcast.4, bf16[128,64,128]{2,1,0:T(8,128)(2,1)} %bitcast.3), custom_call_target="tpu_custom_call" | custom-call | tf_op jit(solution)/shard_map/project/pallas_call | solution.py:335
  3.8 20.5 %all_to_all.5.recv_ref = bf16[8,160,128]{2,1,0:T(8,128)(2,1)S(1)} all-to-all(bf16[8,160,128]{2,1,0:T(8,128)(2,1)S(1)} %project.1), channel_id=1, replica_groups=mesh['dp'=32,'mp'=8] {'mp'}, dimensions={0} | all-to-all | bytes 655360 | tf_op jit(solution)/shard_map/all_to_all | solution.py:355
  24.4 0.5 gram.1
  24.9 2.6 %collective-permute-start = (bf16[304,128]{1,0:T(8,128)(2,1)S(1)}, bf16[304,128]{1,0:T(8,128)(2,1)S(1)}, u32[]{:S(2)}, u32[]{:S(2)}) collective-permute-start(bf16[304,128]{1,0:T(8,128)(2,1)S(1)} %get-tuple-element.10), channel_id=1, source_target_pairs={{0,8},{8,0},{16,24},{24,16},{32,40},{40,32},{48,56},{56,48},{64,72... | collective-permute-start | bytes 233480 | tf_op jit(solution)/shard_map/ppermute | solution.py:378
  27.5 0.9 %collective-permute-done = bf16[304,128]{1,0:T(8,128)(2,1)S(1)} collective-permute-done((bf16[304,128]{1,0:T(8,128)(2,1)S(1)}, bf16[304,128]{1,0:T(8,128)(2,1)S(1)}, u32[]{:S(2)}, u32[]{:S(2)}) %collective-permute-start) | collective-permute-done | bytes 77856 | tf_op jit(solution)/shard_map/ppermute | solution.py:378
  28.4 2.6 %collective-permute-start.3 = (bf16[304,128]{1,0:T(8,128)(2,1)S(1)}, bf16[304,128]{1,0:T(8,128)(2,1)S(1)}, u32[]{:S(2)}, u32[]{:S(2)}) collective-permute-start(bf16[304,128]{1,0:T(8,128)(2,1)S(1)} %add.21), channel_id=1, source_target_pairs={{0,48},{8,56},{16,0},{24,8},{32,16},{40,24},{48,32},{56,40},{64,11... | collective-permute-start | bytes 233480 | tf_op jit(solution)/shard_map/ppermute | solution.py:381
  31.0 0.0 collective-permute-start.2
  31.0 1.7 %collective-permute-start.1 = (bf16[304,128]{1,0:T(8,128)(2,1)S(1)}, bf16[304,128]{1,0:T(8,128)(2,1)S(1)}, u32[]{:S(2)}, u32[]{:S(2)}) collective-permute-start(bf16[304,128]{1,0:T(8,128)(2,1)S(1)} %add.21), channel_id=1, source_target_pairs={{0,32},{8,40},{16,48},{24,56},{32,0},{40,8},{48,16},{56,24},{64,96... | collective-permute-start | bytes 233480 | tf_op jit(solution)/shard_map/ppermute | solution.py:381
  32.7 0.0 copy-done
  32.7 1.2 %features.1 = bf16[32,4096]{1,0:T(8,128)(2,1)} custom-call(s32[1,256]{1,0:T(1,128)S(1)} %copy-done, bf16[160,128]{1,0:T(8,128)(2,1)S(1)} %get-tuple-element.11.coords_ref), custom_call_target="tpu_custom_call" | custom-call | flops 16777216 | bytes 300000 | tf_op jit(solution)/shard_map/features/pallas_call | solution.py:369
  34.0 0.0 collective-permute-done.3
  34.0 2.6 %collective-permute-done.2 = bf16[304,128]{1,0:T(8,128)(2,1)S(1)} collective-permute-done((bf16[304,128]{1,0:T(8,128)(2,1)S(1)}, bf16[304,128]{1,0:T(8,128)(2,1)S(1)}, u32[]{:S(2)}, u32[]{:S(2)}) %collective-permute-start.2) | collective-permute-done | bytes 77856 | tf_op jit(solution)/shard_map/ppermute | solution.py:381
  36.6 0.3 collective-permute-done.1
  36.9 2.8 %collective-permute-start.6 = (bf16[304,128]{1,0:T(8,128)(2,1)S(1)}, bf16[304,128]{1,0:T(8,128)(2,1)S(1)}, u32[]{:S(2)}, u32[]{:S(2)}) collective-permute-start(bf16[304,128]{1,0:T(8,128)(2,1)S(1)} %add_convert_fusion.1), channel_id=1, source_target_pairs={{0,192},{8,200},{16,208},{24,216},{32,224},{40,232},{48,240},{56,2... | collective-permute-start | bytes 233480 | tf_op jit(solution)/shard_map/ppermute | solution.py:381
  39.7 0.0 collective-permute-start.5
  39.8 1.6 %collective-permute-start.4 = (bf16[304,128]{1,0:T(8,128)(2,1)S(1)}, bf16[304,128]{1,0:T(8,128)(2,1)S(1)}, u32[]{:S(2)}, u32[]{:S(2)}) collective-permute-start(bf16[304,128]{1,0:T(8,128)(2,1)S(1)} %add_convert_fusion.1), channel_id=1, source_target_pairs={{0,128},{8,136},{16,144},{24,152},{32,160},{40,168},{48,176},{56,1... | collective-permute-start | bytes 233480 | tf_op jit(solution)/shard_map/ppermute | solution.py:381
  41.4 0.0 collective-permute-done.6
  41.4 3.6 %collective-permute-done.5 = bf16[304,128]{1,0:T(8,128)(2,1)S(1)} collective-permute-done((bf16[304,128]{1,0:T(8,128)(2,1)S(1)}, bf16[304,128]{1,0:T(8,128)(2,1)S(1)}, u32[]{:S(2)}, u32[]{:S(2)}) %collective-permute-start.5) | collective-permute-done | bytes 77856 | tf_op jit(solution)/shard_map/ppermute | solution.py:381
  45.0 0.0 collective-permute-done.4
  45.1 3.5 %collective-permute-start.7 = (bf16[304,128]{1,0:T(8,128)(2,1)S(1)}, bf16[304,128]{1,0:T(8,128)(2,1)S(1)}, u32[]{:S(2)}, u32[]{:S(2)}) collective-permute-start(bf16[304,128]{1,0:T(8,128)(2,1)S(1)} %add_convert_fusion.total_ref), channel_id=1, source_target_pairs={{0,8},{8,0},{16,24},{24,16},{32,40},{40,32},{48,56},{56,48},{64,72... | collective-permute-start | bytes 233480 | tf_op jit(solution)/shard_map/ppermute | solution.py:384
  48.6 0.9 %collective-permute-done.7.other_ref = bf16[304,128]{1,0:T(8,128)(2,1)S(1)} collective-permute-done((bf16[304,128]{1,0:T(8,128)(2,1)S(1)}, bf16[304,128]{1,0:T(8,128)(2,1)S(1)}, u32[]{:S(2)}, u32[]{:S(2)}) %collective-permute-start.7) | collective-permute-done | bytes 77856 | tf_op jit(solution)/shard_map/ppermute | solution.py:384
  49.5 10.8 %factor.1 = f32[512,512]{1,0:T(8,128)} custom-call(bf16[304,128]{1,0:T(8,128)(2,1)S(1)} %add_convert_fusion.total_ref, bf16[304,128]{1,0:T(8,128)(2,1)S(1)} %collective-permute-done.7.other_ref), custom_call_target="tpu_custom_call" | custom-call | tf_op jit(solution)/shard_map/factor/pallas_call | solution.py:385
  (3 shorter events, 0.1 us)
Async XLA Ops:
  0.6 32.1 %copy-start = (s32[1,256]{1,0:T(1,128)S(1)}, s32[1,256]{1,0:T(1,128)}, u32[]{:S(2)}) copy-start(s32[1,256]{1,0:T(1,128)} %assign_ref.1) | copy-start | bytes 3076
  24.9 3.5 %collective-permute-start = (bf16[304,128]{1,0:T(8,128)(2,1)S(1)}, bf16[304,128]{1,0:T(8,128)(2,1)S(1)}, u32[]{:S(2)}, u32[]{:S(2)}) collective-permute-start(bf16[304,128]{1,0:T(8,128)(2,1)S(1)} %get-tuple-element.10), channel_id=1, source_target_pairs={{0,8},{8,0},{16,24},{24,16},{32,40},{40,32},{48,56},{56,48},{64,72... | collective-permute-start | bytes 233480 | tf_op jit(solution)/shard_map/ppermute | solution.py:378
  28.4 5.5 %collective-permute-start.3 = (bf16[304,128]{1,0:T(8,128)(2,1)S(1)}, bf16[304,128]{1,0:T(8,128)(2,1)S(1)}, u32[]{:S(2)}, u32[]{:S(2)}) collective-permute-start(bf16[304,128]{1,0:T(8,128)(2,1)S(1)} %add.21), channel_id=1, source_target_pairs={{0,48},{8,56},{16,0},{24,8},{32,16},{40,24},{48,32},{56,40},{64,11... | collective-permute-start | bytes 233480 | tf_op jit(solution)/shard_map/ppermute | solution.py:381
  31.0 5.6 %collective-permute-start.2 = (bf16[304,128]{1,0:T(8,128)(2,1)S(1)}, bf16[304,128]{1,0:T(8,128)(2,1)S(1)}, u32[]{:S(2)}, u32[]{:S(2)}) collective-permute-start(bf16[304,128]{1,0:T(8,128)(2,1)S(1)} %add.21), channel_id=1, source_target_pairs={{0,16},{8,24},{16,32},{24,40},{32,48},{40,56},{48,0},{56,8},{64,80... | collective-permute-start | bytes 233480 | tf_op jit(solution)/shard_map/ppermute | solution.py:381
  31.0 5.9 %collective-permute-start.1 = (bf16[304,128]{1,0:T(8,128)(2,1)S(1)}, bf16[304,128]{1,0:T(8,128)(2,1)S(1)}, u32[]{:S(2)}, u32[]{:S(2)}) collective-permute-start(bf16[304,128]{1,0:T(8,128)(2,1)S(1)} %add.21), channel_id=1, source_target_pairs={{0,32},{8,40},{16,48},{24,56},{32,0},{40,8},{48,16},{56,24},{64,96... | collective-permute-start | bytes 233480 | tf_op jit(solution)/shard_map/ppermute | solution.py:381
  36.9 4.5 %collective-permute-start.6 = (bf16[304,128]{1,0:T(8,128)(2,1)S(1)}, bf16[304,128]{1,0:T(8,128)(2,1)S(1)}, u32[]{:S(2)}, u32[]{:S(2)}) collective-permute-start(bf16[304,128]{1,0:T(8,128)(2,1)S(1)} %add_convert_fusion.1), channel_id=1, source_target_pairs={{0,192},{8,200},{16,208},{24,216},{32,224},{40,232},{48,240},{56,2... | collective-permute-start | bytes 233480 | tf_op jit(solution)/shard_map/ppermute | solution.py:381
  39.7 5.3 %collective-permute-start.5 = (bf16[304,128]{1,0:T(8,128)(2,1)S(1)}, bf16[304,128]{1,0:T(8,128)(2,1)S(1)}, u32[]{:S(2)}, u32[]{:S(2)}) collective-permute-start(bf16[304,128]{1,0:T(8,128)(2,1)S(1)} %add_convert_fusion.1), channel_id=1, source_target_pairs={{0,64},{8,72},{16,80},{24,88},{32,96},{40,104},{48,112},{56,120},{... | collective-permute-start | bytes 233480 | tf_op jit(solution)/shard_map/ppermute | solution.py:381
  39.8 5.3 %collective-permute-start.4 = (bf16[304,128]{1,0:T(8,128)(2,1)S(1)}, bf16[304,128]{1,0:T(8,128)(2,1)S(1)}, u32[]{:S(2)}, u32[]{:S(2)}) collective-permute-start(bf16[304,128]{1,0:T(8,128)(2,1)S(1)} %add_convert_fusion.1), channel_id=1, source_target_pairs={{0,128},{8,136},{16,144},{24,152},{32,160},{40,168},{48,176},{56,1... | collective-permute-start | bytes 233480 | tf_op jit(solution)/shard_map/ppermute | solution.py:381
  45.1 4.4 %collective-permute-start.7 = (bf16[304,128]{1,0:T(8,128)(2,1)S(1)}, bf16[304,128]{1,0:T(8,128)(2,1)S(1)}, u32[]{:S(2)}, u32[]{:S(2)}) collective-permute-start(bf16[304,128]{1,0:T(8,128)(2,1)S(1)} %add_convert_fusion.total_ref), channel_id=1, source_target_pairs={{0,8},{8,0},{16,24},{24,16},{32,40},{40,32},{48,56},{56,48},{64,72... | collective-permute-start | bytes 233480 | tf_op jit(solution)/shard_map/ppermute | solution.py:384

commit v8 on v7

--- a/solution.py
+++ b/solution.py
@@ -22,7 +22,7 @@
                    index, assign, acts, grads, proj, vals, holder, sems, val_sems):
     me = lax.axis_index("mp")
     k_in = acts.shape[1]
-    k_half = grads.shape[1] // 2
+    cuts = (0, 2560, grads.shape[1])
     blocks = val_sems.shape[0]
     in_copies = (
         pltpu.make_async_copy(index_hbm, index, sems.at[0]),
@@ -31,8 +31,7 @@
         pltpu.make_async_copy(assign_hbm, assign, sems.at[3]),
     )
     out_copies = [
-        pltpu.make_async_copy(grads_hbm.at[:, k_half * n:k_half * n + k_half],
-                              grads.at[:, k_half * n:k_half * n + k_half], sems.at[4 + n])
+        pltpu.make_async_copy(grads_hbm.at[:, cuts[n]:cuts[n + 1]], grads.at[:, cuts[n]:cuts[n + 1]], sems.at[4 + n])
         for n in range(2)
     ]
     for copy in (*in_copies, *out_copies):
@@ -74,9 +73,9 @@
             value_copy(j).wait()
 
     out_copies[0].wait()
-    out_part = nt_dot(vals[:, 0:k_half], grads[:, 0:k_half])
+    out_part = nt_dot(vals[:, 0:cuts[1]], grads[:, 0:cuts[1]])
     out_copies[1].wait()
-    out_part = out_part + nt_dot(vals[:, k_half:2 * k_half], grads[:, k_half:2 * k_half])
+    out_part = out_part + nt_dot(vals[:, cuts[1]:], grads[:, cuts[1]:])
     out_part = out_part.astype(BF16)
     for c in range(send_ref.shape[0]):
         send_ref[c, 0:64, :] = out_part[:, 0:128]
@@ -187,7 +186,7 @@
 WIDE = 16
 
 
-def factor_block(c):
+def factor_block(c, invert):
     sub = lax.broadcasted_iota(jnp.int32, (8, 128), 0)
     lane = lax.broadcasted_iota(jnp.int32, (8, 128), 1)
     n = len(c)
@@ -201,6 +200,8 @@
         if p:
             cols[0][0] = cols[0][0] + 0.0 * (cols[WIDE - 1][h - 1] + cols[WIDE - 2][h - 1])
         aug = [jnp.where(inside, jnp.where(lane - base == sub + 8 * u, 1.0, 0.0), own[u]) for u in range(h)]
+        if not invert:
+            aug = list(own)
         zed = list(aug)
         near = range(p + h, min(p + 2 * h, n))
         below = {t: [spread_lane(c[t], base + k) for k in range(WIDE)] for t in near}
@@ -224,7 +225,8 @@
                 if u >= v:
                     low = part if u == v else m[u]
                     own[u] = own[u] - low * ro
-                    aug[u] = aug[u] - low * ra
+                    if invert:
+                        aug[u] = aug[u] - low * ra
                 zed[u] = zed[u] - m[u] * rz
         rows, dones = [], []
         for u in range(h):
@@ -296,12 +298,13 @@
     for s in range(4):
         o = place[s, s]
         c = [work[o + 8 * t:o + 8 * t + 8, :] + jnp.where(lane == sub + 8 * t, DAMPING, 0.0) for t in range(16)]
-        upper, inverse = factor_block(c)
+        upper, inverse = factor_block(c, s < 3)
         if s:
             done[s - 1].start()
         for t in range(16):
             out[128 * s + 8 * t:128 * s + 8 * t + 8, 128 * s:128 * s + 128] = upper[t]
-            inv[8 * t:8 * t + 8, :] = inverse[t]
+            if s < 3:
+                inv[8 * t:8 * t + 8, :] = inverse[t]
         for j in range(s):
             out[128 * s:128 * s + 128, 128 * j:128 * j + 128] = jnp.zeros((128, 128), F32)
         for j in range(s + 1, 4):

time: 60.7 us -> 60.7 us (level)
  no operation moved by 1% of the time
where the time goes in v8:
time: 60.7 us; the launch traced here: 60.5 us
  blocking collectives  20.6 us (34%)
  Pallas kernels  15.8 us (26%)
  starting transfers between devices  14.8 us (24%)
  waiting for transfers between devices  8.4 us (14%)
  between operations  0.83 us (1%)
    all_to_all x1, blocking collectives, shards(): recv = lax.all_to_all(send, 'mp', 0, 0, tiled=True)  20.6 us
    pallas_call x1, Pallas kernels, shards(): pl.pallas_call(factor_kernel, out_shape=jax.ShapeDtypeStruct((FB, FB), F3...  10.8 us
    ppermute x6, starting transfers between devices, shards(): lax.ppermute(total, 'dp', moves(functools.partial(ring, k=k))).astype(F32)  8.75 us
    ppermute x6, waiting for transfers between devices, shards(): lax.ppermute(total, 'dp', moves(functools.partial(ring, k=k))).astype(F32)  6.57 us
    ppermute x1, starting transfers between devices, shards(): other = lax.ppermute(total, 'dp', moves(lambda y, x, c: (y, x, 1 - c)))  3.47 us
    pallas_call x1, Pallas kernels, shards(): pl.pallas_call(project_kernel, out_shape=jax.ShapeDtypeStruct((8, 160, 12...  3.25 us
    ppermute x1, starting transfers between devices, shards(): lax.ppermute(give, 'dp', moves(lambda y, x, c: (y, x, 1 - c)))  2.54 us
    pallas_call x1, Pallas kernels, shards(): pl.pallas_call(features_kernel, out_shape=jax.ShapeDtypeStruct((32, 4096)...  1.22 us
  transfers between devices with their start and end apart: 8, of which 5 were waited for; matrix products, arithmetic and copies ran while one was open for 0% of the time, Pallas kernels for 2%

profile of v8, /device:TPU:1, one launch (start us, length us, event | category | flops | bytes accessed | tf_op | source)
XLA Modules:
  0.0 60.5 jit_solution(17622293493982589563)
XLA Ops:
  0.6 0.0 copy-start
  0.6 3.2 %project.1 = bf16[8,160,128]{2,1,0:T(8,128)(2,1)S(1)} custom-call(s32[128]{0:T(128)} %index_hbm.1, s32[1,256]{1,0:T(1,128)} %assign_ref.1, bf16[256,1024]{1,0:T(8,128)(2,1)} %acts_hbm.1, bf16[256,3584]{1,0:T(8,128)(2,1)} %grads_hbm.1, bf16[64,8192]{1,0:T(8,128)(2,1)} %bitcast.4, bf16[128,64,128]{2,1,0:T(8,128)(2,1)} %bitcast.3), custom_call_target="tpu_custom_call" | custom-call | tf_op jit(solution)/shard_map/project/pallas_call | solution.py:338
  3.9 20.6 %all_to_all.5.recv_ref = bf16[8,160,128]{2,1,0:T(8,128)(2,1)S(1)} all-to-all(bf16[8,160,128]{2,1,0:T(8,128)(2,1)S(1)} %project.1), channel_id=1, replica_groups=mesh['dp'=32,'mp'=8] {'mp'}, dimensions={0} | all-to-all | bytes 655360 | tf_op jit(solution)/shard_map/all_to_all | solution.py:358
  24.5 0.5 gram.1
  25.0 2.5 %collective-permute-start = (bf16[304,128]{1,0:T(8,128)(2,1)S(1)}, bf16[304,128]{1,0:T(8,128)(2,1)S(1)}, u32[]{:S(2)}, u32[]{:S(2)}) collective-permute-start(bf16[304,128]{1,0:T(8,128)(2,1)S(1)} %get-tuple-element.10), channel_id=1, source_target_pairs={{0,8},{8,0},{16,24},{24,16},{32,40},{40,32},{48,56},{56,48},{64,72... | collective-permute-start | bytes 233480 | tf_op jit(solution)/shard_map/ppermute | solution.py:381
  27.5 0.9 %collective-permute-done = bf16[304,128]{1,0:T(8,128)(2,1)S(1)} collective-permute-done((bf16[304,128]{1,0:T(8,128)(2,1)S(1)}, bf16[304,128]{1,0:T(8,128)(2,1)S(1)}, u32[]{:S(2)}, u32[]{:S(2)}) %collective-permute-start) | collective-permute-done | bytes 77856 | tf_op jit(solution)/shard_map/ppermute | solution.py:381
  28.5 2.6 %collective-permute-start.3 = (bf16[304,128]{1,0:T(8,128)(2,1)S(1)}, bf16[304,128]{1,0:T(8,128)(2,1)S(1)}, u32[]{:S(2)}, u32[]{:S(2)}) collective-permute-start(bf16[304,128]{1,0:T(8,128)(2,1)S(1)} %add.21), channel_id=1, source_target_pairs={{0,48},{8,56},{16,0},{24,8},{32,16},{40,24},{48,32},{56,40},{64,11... | collective-permute-start | bytes 233480 | tf_op jit(solution)/shard_map/ppermute | solution.py:384
  31.0 0.0 collective-permute-start.2
  31.0 1.7 %collective-permute-start.1 = (bf16[304,128]{1,0:T(8,128)(2,1)S(1)}, bf16[304,128]{1,0:T(8,128)(2,1)S(1)}, u32[]{:S(2)}, u32[]{:S(2)}) collective-permute-start(bf16[304,128]{1,0:T(8,128)(2,1)S(1)} %add.21), channel_id=1, source_target_pairs={{0,32},{8,40},{16,48},{24,56},{32,0},{40,8},{48,16},{56,24},{64,96... | collective-permute-start | bytes 233480 | tf_op jit(solution)/shard_map/ppermute | solution.py:384
  32.8 0.0 copy-done
  32.8 1.2 %features.1 = bf16[32,4096]{1,0:T(8,128)(2,1)} custom-call(s32[1,256]{1,0:T(1,128)S(1)} %copy-done, bf16[160,128]{1,0:T(8,128)(2,1)S(1)} %get-tuple-element.11.coords_ref), custom_call_target="tpu_custom_call" | custom-call | flops 16777216 | bytes 300000 | tf_op jit(solution)/shard_map/features/pallas_call | solution.py:372
  34.0 0.0 collective-permute-done.3
  34.0 2.6 %collective-permute-done.2 = bf16[304,128]{1,0:T(8,128)(2,1)S(1)} collective-permute-done((bf16[304,128]{1,0:T(8,128)(2,1)S(1)}, bf16[304,128]{1,0:T(8,128)(2,1)S(1)}, u32[]{:S(2)}, u32[]{:S(2)}) %collective-permute-start.2) | collective-permute-done | bytes 77856 | tf_op jit(solution)/shard_map/ppermute | solution.py:384
  36.6 0.3 collective-permute-done.1
  37.0 2.8 %collective-permute-start.6 = (bf16[304,128]{1,0:T(8,128)(2,1)S(1)}, bf16[304,128]{1,0:T(8,128)(2,1)S(1)}, u32[]{:S(2)}, u32[]{:S(2)}) collective-permute-start(bf16[304,128]{1,0:T(8,128)(2,1)S(1)} %add_convert_fusion.1), channel_id=1, source_target_pairs={{0,192},{8,200},{16,208},{24,216},{32,224},{40,232},{48,240},{56,2... | collective-permute-start | bytes 233480 | tf_op jit(solution)/shard_map/ppermute | solution.py:384
  39.8 0.0 collective-permute-start.5
  39.8 1.6 %collective-permute-start.4 = (bf16[304,128]{1,0:T(8,128)(2,1)S(1)}, bf16[304,128]{1,0:T(8,128)(2,1)S(1)}, u32[]{:S(2)}, u32[]{:S(2)}) collective-permute-start(bf16[304,128]{1,0:T(8,128)(2,1)S(1)} %add_convert_fusion.1), channel_id=1, source_target_pairs={{0,128},{8,136},{16,144},{24,152},{32,160},{40,168},{48,176},{56,1... | collective-permute-start | bytes 233480 | tf_op jit(solution)/shard_map/ppermute | solution.py:384
  41.4 0.0 collective-permute-done.6
  41.4 3.6 %collective-permute-done.5 = bf16[304,128]{1,0:T(8,128)(2,1)S(1)} collective-permute-done((bf16[304,128]{1,0:T(8,128)(2,1)S(1)}, bf16[304,128]{1,0:T(8,128)(2,1)S(1)}, u32[]{:S(2)}, u32[]{:S(2)}) %collective-permute-start.5) | collective-permute-done | bytes 77856 | tf_op jit(solution)/shard_map/ppermute | solution.py:384
  45.1 0.0 collective-permute-done.4
  45.1 3.5 %collective-permute-start.7 = (bf16[304,128]{1,0:T(8,128)(2,1)S(1)}, bf16[304,128]{1,0:T(8,128)(2,1)S(1)}, u32[]{:S(2)}, u32[]{:S(2)}) collective-permute-start(bf16[304,128]{1,0:T(8,128)(2,1)S(1)} %add_convert_fusion.total_ref), channel_id=1, source_target_pairs={{0,8},{8,0},{16,24},{24,16},{32,40},{40,32},{48,56},{56,48},{64,72... | collective-permute-start | bytes 233480 | tf_op jit(solution)/shard_map/ppermute | solution.py:387
  48.6 0.9 %collective-permute-done.7.other_ref = bf16[304,128]{1,0:T(8,128)(2,1)S(1)} collective-permute-done((bf16[304,128]{1,0:T(8,128)(2,1)S(1)}, bf16[304,128]{1,0:T(8,128)(2,1)S(1)}, u32[]{:S(2)}, u32[]{:S(2)}) %collective-permute-start.7) | collective-permute-done | bytes 77856 | tf_op jit(solution)/shard_map/ppermute | solution.py:387
  49.5 10.8 %factor.1 = f32[512,512]{1,0:T(8,128)} custom-call(bf16[304,128]{1,0:T(8,128)(2,1)S(1)} %add_convert_fusion.total_ref, bf16[304,128]{1,0:T(8,128)(2,1)S(1)} %collective-permute-done.7.other_ref), custom_call_target="tpu_custom_call" | custom-call | tf_op jit(solution)/shard_map/factor/pallas_call | solution.py:388
  (3 shorter events, 0.1 us)
Async XLA Ops:
  0.6 32.2 %copy-start = (s32[1,256]{1,0:T(1,128)S(1)}, s32[1,256]{1,0:T(1,128)}, u32[]{:S(2)}) copy-start(s32[1,256]{1,0:T(1,128)} %assign_ref.1) | copy-start | bytes 3076
  25.0 3.5 %collective-permute-start = (bf16[304,128]{1,0:T(8,128)(2,1)S(1)}, bf16[304,128]{1,0:T(8,128)(2,1)S(1)}, u32[]{:S(2)}, u32[]{:S(2)}) collective-permute-start(bf16[304,128]{1,0:T(8,128)(2,1)S(1)} %get-tuple-element.10), channel_id=1, source_target_pairs={{0,8},{8,0},{16,24},{24,16},{32,40},{40,32},{48,56},{56,48},{64,72... | collective-permute-start | bytes 233480 | tf_op jit(solution)/shard_map/ppermute | solution.py:381
  28.5 5.5 %collective-permute-start.3 = (bf16[304,128]{1,0:T(8,128)(2,1)S(1)}, bf16[304,128]{1,0:T(8,128)(2,1)S(1)}, u32[]{:S(2)}, u32[]{:S(2)}) collective-permute-start(bf16[304,128]{1,0:T(8,128)(2,1)S(1)} %add.21), channel_id=1, source_target_pairs={{0,48},{8,56},{16,0},{24,8},{32,16},{40,24},{48,32},{56,40},{64,11... | collective-permute-start | bytes 233480 | tf_op jit(solution)/shard_map/ppermute | solution.py:384
  31.0 5.6 %collective-permute-start.2 = (bf16[304,128]{1,0:T(8,128)(2,1)S(1)}, bf16[304,128]{1,0:T(8,128)(2,1)S(1)}, u32[]{:S(2)}, u32[]{:S(2)}) collective-permute-start(bf16[304,128]{1,0:T(8,128)(2,1)S(1)} %add.21), channel_id=1, source_target_pairs={{0,16},{8,24},{16,32},{24,40},{32,48},{40,56},{48,0},{56,8},{64,80... | collective-permute-start | bytes 233480 | tf_op jit(solution)/shard_map/ppermute | solution.py:384
  31.0 5.9 %collective-permute-start.1 = (bf16[304,128]{1,0:T(8,128)(2,1)S(1)}, bf16[304,128]{1,0:T(8,128)(2,1)S(1)}, u32[]{:S(2)}, u32[]{:S(2)}) collective-permute-start(bf16[304,128]{1,0:T(8,128)(2,1)S(1)} %add.21), channel_id=1, source_target_pairs={{0,32},{8,40},{16,48},{24,56},{32,0},{40,8},{48,16},{56,24},{64,96... | collective-permute-start | bytes 233480 | tf_op jit(solution)/shard_map/ppermute | solution.py:384
  37.0 4.5 %collective-permute-start.6 = (bf16[304,128]{1,0:T(8,128)(2,1)S(1)}, bf16[304,128]{1,0:T(8,128)(2,1)S(1)}, u32[]{:S(2)}, u32[]{:S(2)}) collective-permute-start(bf16[304,128]{1,0:T(8,128)(2,1)S(1)} %add_convert_fusion.1), channel_id=1, source_target_pairs={{0,192},{8,200},{16,208},{24,216},{32,224},{40,232},{48,240},{56,2... | collective-permute-start | bytes 233480 | tf_op jit(solution)/shard_map/ppermute | solution.py:384
  39.8 5.3 %collective-permute-start.5 = (bf16[304,128]{1,0:T(8,128)(2,1)S(1)}, bf16[304,128]{1,0:T(8,128)(2,1)S(1)}, u32[]{:S(2)}, u32[]{:S(2)}) collective-permute-start(bf16[304,128]{1,0:T(8,128)(2,1)S(1)} %add_convert_fusion.1), channel_id=1, source_target_pairs={{0,64},{8,72},{16,80},{24,88},{32,96},{40,104},{48,112},{56,120},{... | collective-permute-start | bytes 233480 | tf_op jit(solution)/shard_map/ppermute | solution.py:384
  39.8 5.3 %collective-permute-start.4 = (bf16[304,128]{1,0:T(8,128)(2,1)S(1)}, bf16[304,128]{1,0:T(8,128)(2,1)S(1)}, u32[]{:S(2)}, u32[]{:S(2)}) collective-permute-start(bf16[304,128]{1,0:T(8,128)(2,1)S(1)} %add_convert_fusion.1), channel_id=1, source_target_pairs={{0,128},{8,136},{16,144},{24,152},{32,160},{40,168},{48,176},{56,1... | collective-permute-start | bytes 233480 | tf_op jit(solution)/shard_map/ppermute | solution.py:384
  45.1 4.4 %collective-permute-start.7 = (bf16[304,128]{1,0:T(8,128)(2,1)S(1)}, bf16[304,128]{1,0:T(8,128)(2,1)S(1)}, u32[]{:S(2)}, u32[]{:S(2)}) collective-permute-start(bf16[304,128]{1,0:T(8,128)(2,1)S(1)} %add_convert_fusion.total_ref), channel_id=1, source_target_pairs={{0,8},{8,0},{16,24},{24,16},{32,40},{40,32},{48,56},{56,48},{64,72... | collective-permute-start | bytes 233480 | tf_op jit(solution)/shard_map/ppermute | solution.py:387
